TPU v7x, 32 devices: a whole 2x2x4 slice. The times are simulated.
32 devices in a mesh: wide: 8 (over z, y), narrow: 4 (over x, core).
Axes of the slice: x: 2, y: 2, z: 4, core: 2. Of those that a mesh axis runs over, the one named last changes fastest.
Arguments:
- stream: bfloat16 [1024, 2048], P('wide', 'narrow'), may hold values from -6 to 6
- out_grad: bfloat16 [1024, 2048], P('wide', 'narrow'), may hold values from -6 to 6
- attn_gain: bfloat16 [2048], P('wide'), may hold values from 0.099609375 to 1.8984375
- attn_router: bfloat16 [2048, 4], P('wide'), may hold values from -0.125 to 0.125
- key_value: bfloat16 [2, 2048, 2048], P(None, 'wide', 'narrow'), may hold values from -0.125 to 0.125
- query_proj: bfloat16 [4, 2048, 2048], P(None, 'wide', 'narrow'), may hold values from -0.1875 to 0.1875
- output_proj: bfloat16 [4, 2048, 2048], P(None, 'wide', 'narrow'), may hold values from -0.5 to 0.5
- mlp_gain: bfloat16 [2048], P('wide'), may hold values from 0.099609375 to 1.8984375
- mlp_router: bfloat16 [2048, 4], P('wide'), may hold values from -0.125 to 0.125
- expert_in: bfloat16 [8, 2048, 2, 2816], P('wide', None, None, 'narrow'), may hold values from -0.125 to 0.125
- expert_down: bfloat16 [8, 2816, 2048], P('wide', 'narrow'), may hold values from -0.15625 to 0.15625
- attn_routes: int32 [1024, 2], P('wide'), may hold values from 0 to 3, all different within a row; in each aligned block of 128 rows (0 to 127, 128 to 255, ...) at most 80 rows name the same one
- mlp_routes: int32 [1024, 2], P('wide'), may hold values from 0 to 3, all different within a row; in each aligned block of 128 rows (0 to 127, 128 to 255, ...) at most 80 rows name the same one
- doc_lengths: int32 [8, 4], P('wide'), may hold values from 1 to 96, 128 in all within a row
Outputs:
- layer_out: float32 [1024, 2048], P('wide', 'narrow')
- stream_grad: float32 [1024, 2048], P('wide', 'narrow')
- attn_gain_grad: float32 [2048], P('wide')
- attn_router_grad: float32 [2048, 4], P('wide')
- key_value_grad: float32 [2, 2048, 2048], P(None, 'wide', 'narrow')
- query_grad: float32 [4, 2048, 2048], P(None, 'wide', 'narrow')
- output_grad: float32 [4, 2048, 2048], P(None, 'wide', 'narrow')
- mlp_gain_grad: float32 [2048], P('wide')
- mlp_router_grad: float32 [2048, 4], P('wide')
- expert_in_grad: float32 [8, 2048, 2, 2816], P('wide', None, None, 'narrow')
- expert_down_grad: float32 [8, 2816, 2048], P('wide', 'narrow')
Inputs may be any that keep to these rules, and one draw needn't show every extreme that they name: `attn_routes`: the 2 experts of a token differ. Among the 128 tokens of one block no expert is named more than 80 times, a bound that some block reaches. `mlp_routes`: as for attn_routes. `doc_lengths`: row b holds, in order, the lengths of the documents packed into tokens b * 128 to (b + 1) * 128 - 1; each row sums to 128.
All inputs are finite; a program needn't handle non-finite values.
Results may differ from a plain program's by a relative error of at most 0.019.
Values may be sent and summed in bfloat16 or wider, within the bound.
No kernel may reach another device: no remote copies, remote signals or barrier semaphores. Data moves between devices by JAX's collectives and lax.ppermute only.
A program may use at most 256 MiB of HBM per device.

v0:
```python
import jax
import jax.numpy as jnp
from jax import lax
from jax.sharding import PartitionSpec as P

D = 2048
HS = 128
E = 4
TOPK = 2
TOK = 128
SLOTS = 80


EPSILON = 1e-05
NEGATIVE = -1000000000.0
PRECISE = lax.Precision.HIGHEST


def prefix_2(part, axis, combine, identity):
    place = lax.axis_index(axis)
    gathered = lax.all_gather(part, axis)
    state = jnp.zeros_like(part) + jnp.asarray(identity, part.dtype)

    def one(hop, state):
        return combine(state, lax.dynamic_index_in_dim(gathered, hop, 0, False))

    return lax.fori_loop(0, place, one, state)


def rms_scale(values):
    return lax.rsqrt(jnp.mean(values * values, axis=-1) + EPSILON)


def local_places(routes):
    flat_routes = routes.reshape(-1)
    one_hot = (flat_routes[:, None] == jnp.arange(E, dtype=jnp.int32)[None, :]).astype(jnp.int32)
    before = jnp.cumsum(one_hot, axis=0) - one_hot
    return (flat_routes, jnp.sum(before * one_hot, axis=1), jnp.sum(one_hot, axis=0))


def lookup(flat_routes, table):
    chosen = flat_routes[:, None] == jnp.arange(E, dtype=jnp.int32)[None, :]
    return jnp.sum(jnp.where(chosen, table[None, :], 0), axis=1)


def route_hot(routes):
    return (routes[:, :, None] == jnp.arange(E, dtype=jnp.int32)[None, None, :]).astype(jnp.float32)


def chosen_gates(logits, route_mask, keep_mask):
    picked = jnp.sum(route_mask * logits[:, None, :], axis=-1)
    return (jax.nn.softmax(picked, axis=-1), keep_mask.reshape(picked.shape).astype(jnp.float32))


def gate_back(prob_vals, dprob_vals, route_mask):
    dselect = prob_vals * (dprob_vals - jnp.sum(prob_vals * dprob_vals, axis=-1, keepdims=True))
    return jnp.sum(route_mask * dselect[:, :, None], axis=1)


def to_slots(values, slot_index):
    empty = jnp.zeros((E * SLOTS,) + values.shape[1:], values.dtype)
    return empty.at[slot_index].set(values, mode="drop")


def from_slots(buffer, slot_index):
    return jnp.take(buffer, slot_index, axis=0, mode="fill", fill_value=0)


def spread(buffer, sub_count):
    shaped = buffer.reshape((E, 1, SLOTS) + buffer.shape[1:])
    shaped = jnp.broadcast_to(shaped, (E, sub_count, SLOTS) + buffer.shape[1:])
    return shaped.reshape((E * sub_count, SLOTS) + buffer.shape[1:])


def collect(received, sub_count):
    shaped = received.reshape((E, sub_count, SLOTS) + received.shape[2:])
    return jnp.sum(shaped, axis=1).reshape((E * SLOTS,) + received.shape[2:])


def doc_mask(lengths):
    doc_ends = jnp.cumsum(lengths)
    positions = jnp.arange(TOK, dtype=jnp.int32)
    member = jnp.sum((positions[:, None] >= doc_ends[None, :]).astype(jnp.int32), axis=1)
    return (member[:, None] == member[None, :]) & (positions[None, :] <= positions[:, None])


def raw_scores(query_rows, key_rows, allowed, score_scale):
    scores = (
        jnp.einsum("rhc,jhc->hrj", query_rows, key_rows, preferred_element_type=jnp.float32)
        * score_scale
    )
    return jnp.where(allowed[None, :, :], scores, NEGATIVE)


def contract_rows(left, right):
    return lax.dot_general(
        left, right, (((0,), (0,)), ((), ())), precision=PRECISE, preferred_element_type=jnp.float32
    )


def contract_cols(left, right):
    return lax.dot_general(
        left, right, (((1,), (1,)), ((), ())), precision=PRECISE, preferred_element_type=jnp.float32
    )


def split_product(form, weighted, other):
    upper = weighted.astype(jnp.bfloat16)
    lower = (weighted - upper.astype(jnp.float32)).astype(jnp.bfloat16)
    return jnp.einsum(form, upper, other, preferred_element_type=jnp.float32) + jnp.einsum(
        form, lower, other, preferred_element_type=jnp.float32
    )


def local(
    stream,
    out_grad,
    attn_gain,
    attn_router,
    key_value,
    query_proj,
    output_proj,
    mlp_gain,
    mlp_router,
    expert_in,
    expert_down,
    attn_routes,
    mlp_routes,
    doc_lengths,
):
    wide_count = lax.axis_size("wide")
    narrow_index = lax.axis_index("narrow")
    part_width = stream.shape[1]
    sub_count = wide_count // E
    capacity = 9 * TOK * wide_count * TOPK // (8 * E)
    head_count = key_value.shape[2] // HS
    local_width = key_value.shape[2]
    score_scale = HS ** (-0.5)
    attn_flat, attn_rank, attn_totals = local_places(attn_routes)
    mlp_flat, mlp_rank, mlp_totals = local_places(mlp_routes)

    def add_counts(earlier, later):
        return earlier + later

    prefix = prefix_2(
        jnp.stack([attn_totals, mlp_totals]), "wide", add_counts, jnp.zeros((2, E), jnp.int32)
    )
    attn_keep = lookup(attn_flat, prefix[0]) + attn_rank < capacity
    mlp_keep = lookup(mlp_flat, prefix[1]) + mlp_rank < capacity
    attn_slot = jnp.where(attn_keep, attn_flat * SLOTS + attn_rank, E * SLOTS)
    mlp_slot = jnp.where(mlp_keep, mlp_flat * SLOTS + mlp_rank, E * SLOTS)
    attn_mask = route_hot(attn_routes)
    mlp_mask = route_hot(mlp_routes)
    allowed = jnp.repeat(doc_mask(doc_lengths[0]), 2, axis=0)
    rows_in, out_full_rows = (
        lax.all_gather(stream, "narrow", axis=1, tiled=True),
        lax.all_gather(out_grad, "narrow", axis=1, tiled=True),
    )
    kv_full, query_full, out_full, gain_one, gain_two, router_one, router_two = (
        lax.all_gather(key_value, "wide", axis=1, tiled=True),
        lax.all_gather(query_proj, "wide", axis=1, tiled=True),
        lax.all_gather(output_proj, "wide", axis=1, tiled=True),
        lax.all_gather(attn_gain, "wide", axis=0, tiled=True),
        lax.all_gather(mlp_gain, "wide", axis=0, tiled=True),
        lax.all_gather(attn_router, "wide", axis=0, tiled=True),
        lax.all_gather(mlp_router, "wide", axis=0, tiled=True),
    )
    stream_full = rows_in.astype(jnp.float32)
    scale_one = rms_scale(stream_full)
    normed_one = stream_full * scale_one[:, None] * gain_one.astype(jnp.float32)
    prob_one, keep_one = chosen_gates(
        jnp.dot(normed_one, router_one.astype(jnp.float32), precision=PRECISE), attn_mask, attn_keep
    )
    gate_one = prob_one * keep_one
    normed_low = normed_one.astype(jnp.bfloat16)
    key_val = jnp.einsum(
        "td,kdh->kth", normed_low, kv_full, preferred_element_type=jnp.float32
    ).astype(jnp.bfloat16)
    key_rows = key_val[0].reshape(TOK, head_count, HS)
    value_rows = key_val[1].reshape(TOK, head_count, HS)
    token_flat = to_slots(jnp.repeat(normed_low, 2, axis=0), attn_slot)
    token_slots = token_flat.reshape(E, SLOTS, D)
    query_slots = jnp.einsum(
        "emd,edh->emh", token_slots, query_full, preferred_element_type=jnp.float32
    ).astype(jnp.bfloat16)
    query_rows = from_slots(query_slots.reshape(E * SLOTS, local_width), attn_slot).reshape(
        TOK * 2, head_count, HS
    )
    scores = raw_scores(query_rows, key_rows, allowed, score_scale)
    top_score = jnp.max(scores, axis=-1)
    exp_scores = jnp.exp(scores - top_score[:, :, None])
    exp_total = jnp.sum(exp_scores, axis=-1)
    soft_weights = exp_scores / exp_total[:, :, None]
    log_total = top_score + jnp.log(exp_total)
    context = (
        jnp.einsum(
            "hrj,jhc->rhc",
            soft_weights.astype(jnp.bfloat16),
            value_rows,
            preferred_element_type=jnp.float32,
        )
        .astype(jnp.bfloat16)
        .reshape(TOK * 2, local_width)
    )
    context_flat = to_slots(context, attn_slot)
    context_slots = context_flat.reshape(E, SLOTS, local_width)
    output_slots = jnp.einsum(
        "emh,edh->emd", context_slots, out_full, preferred_element_type=jnp.float32
    )
    output_pairs = from_slots(output_slots.reshape(E * SLOTS, D), attn_slot).reshape(TOK, 2, D)
    attn_part = jnp.sum(output_pairs * gate_one[:, :, None], axis=1)
    attention = lax.psum(attn_part, "narrow")
    hidden = stream_full + attention
    scale_two = rms_scale(hidden)
    gain_twof = gain_two.astype(jnp.float32)
    router_twof = router_two.astype(jnp.float32)
    normed_two = hidden * scale_two[:, None] * gain_twof
    prob_two, keep_two = chosen_gates(
        jnp.dot(normed_two, router_twof, precision=PRECISE), mlp_mask, mlp_keep
    )
    gate_two = prob_two * keep_two
    send_rows = spread(
        to_slots(jnp.repeat(normed_two.astype(jnp.bfloat16), 2, axis=0), mlp_slot), sub_count
    )
    expert_rows = lax.all_to_all(
        send_rows, "wide", split_axis=0, concat_axis=0, tiled=True
    ).reshape(-1, D)
    weight_up = expert_in[0]
    weight_down = expert_down[0]
    gate_up = jnp.einsum("rd,dkf->rkf", expert_rows, weight_up, preferred_element_type=jnp.float32)
    gate_pre = gate_up[:, 0]
    up_pre = gate_up[:, 1]
    gate_sig = jax.nn.sigmoid(gate_pre)
    silu_gate = gate_pre * gate_sig
    activation = (silu_gate * up_pre).astype(jnp.bfloat16)
    partial_out = jnp.dot(activation, weight_down, preferred_element_type=jnp.float32)
    returned = lax.all_to_all(
        partial_out.reshape(wide_count, SLOTS, D), "wide", split_axis=0, concat_axis=0, tiled=True
    )
    expert_pairs = from_slots(collect(returned, sub_count), mlp_slot).reshape(TOK, 2, D)
    moe_part = jnp.sum(expert_pairs * gate_two[:, :, None], axis=1)
    mixture = lax.psum_scatter(
        moe_part.astype(jnp.bfloat16), "narrow", scatter_dimension=1, tiled=True
    ).astype(jnp.float32)
    layer_out = lax.dynamic_slice_in_dim(hidden, narrow_index * part_width, part_width, 1) + mixture
    out_rows = out_full_rows.astype(jnp.float32)
    dprob_part_two = keep_two * jnp.sum(expert_pairs * out_rows[:, None, :], axis=-1)
    grad_pairs = (gate_two.reshape(-1)[:, None] * jnp.repeat(out_rows, 2, axis=0)).astype(
        jnp.bfloat16
    )
    grad_rows = lax.all_to_all(
        spread(to_slots(grad_pairs, mlp_slot), sub_count),
        "wide",
        split_axis=0,
        concat_axis=0,
        tiled=True,
    ).reshape(-1, D)
    down_grad = lax.dot_general(
        activation, grad_rows, (((0,), (0,)), ((), ())), preferred_element_type=jnp.float32
    )
    dactiv = lax.dot_general(
        grad_rows, weight_down, (((1,), (1,)), ((), ())), preferred_element_type=jnp.float32
    )
    dgate_pre = (dactiv * up_pre * gate_sig * (1.0 + gate_pre * (1.0 - gate_sig))).astype(
        jnp.bfloat16
    )
    dup_pre = (dactiv * silu_gate).astype(jnp.bfloat16)
    dboth = jnp.stack([dgate_pre, dup_pre], axis=1)
    up_grad = jnp.einsum("rd,rkf->dkf", expert_rows, dboth, preferred_element_type=jnp.float32)
    drows_back = jnp.einsum("rkf,dkf->rd", dboth, weight_up, preferred_element_type=jnp.float32)
    grad_back = lax.all_to_all(
        drows_back.reshape(wide_count, SLOTS, D), "wide", split_axis=0, concat_axis=0, tiled=True
    )
    dnormed_part = jnp.sum(
        from_slots(collect(grad_back, sub_count), mlp_slot).reshape(TOK, 2, D), axis=1
    )
    dnormed_two, dprob_two = lax.psum((dnormed_part, dprob_part_two), "narrow")
    dlogit_two = gate_back(prob_two, dprob_two, mlp_mask)
    dnormed_two = dnormed_two + contract_cols(dlogit_two, router_twof)
    gain_two_term = dnormed_two * hidden * scale_two[:, None]
    gained_two = dnormed_two * gain_twof
    inner_two = jnp.sum(gained_two * hidden, axis=-1)
    dhidden = (
        out_rows
        + scale_two[:, None] * gained_two
        - hidden * (scale_two**3 * inner_two / D)[:, None]
    )
    dhidden_low = dhidden.astype(jnp.bfloat16)
    dprob_part_one = keep_one * jnp.sum(
        output_pairs * dhidden_low.astype(jnp.float32)[:, None, :], axis=-1
    )
    grad_flat = to_slots(jnp.repeat(dhidden_low, 2, axis=0), attn_slot)
    grad_slots = grad_flat.reshape(E, SLOTS, D)
    dcontext_slots = jnp.einsum(
        "emd,edh->emh", grad_slots, out_full, preferred_element_type=jnp.float32
    )
    dcontext = (
        from_slots(dcontext_slots.reshape(E * SLOTS, local_width), attn_slot)
        * gate_one.reshape(-1)[:, None]
    ).astype(jnp.bfloat16)
    dcontext_rows = dcontext.reshape(TOK * 2, head_count, HS)
    again_weights = jnp.exp(
        raw_scores(query_rows, key_rows, allowed, score_scale) - log_total[:, :, None]
    )
    dweights = jnp.einsum(
        "rhc,jhc->hrj", dcontext_rows, value_rows, preferred_element_type=jnp.float32
    )
    row_delta = jnp.sum(again_weights * dweights, axis=-1)
    dscores = (again_weights * (dweights - row_delta[:, :, None])).astype(jnp.bfloat16)
    dquery = (
        (
            jnp.einsum("hrj,jhc->rhc", dscores, key_rows, preferred_element_type=jnp.float32)
            * score_scale
        )
        .astype(jnp.bfloat16)
        .reshape(TOK * 2, local_width)
    )
    dkeys = (
        (
            jnp.einsum("hrj,rhc->jhc", dscores, query_rows, preferred_element_type=jnp.float32)
            * score_scale
        )
        .astype(jnp.bfloat16)
        .reshape(TOK, local_width)
    )
    dvalues = (
        jnp.einsum(
            "hrj,rhc->jhc",
            again_weights.astype(jnp.bfloat16),
            dcontext_rows,
            preferred_element_type=jnp.float32,
        )
        .astype(jnp.bfloat16)
        .reshape(TOK, local_width)
    )
    dkey_val = jnp.stack([dkeys, dvalues])
    dquery_flat = to_slots(dquery, attn_slot)
    dquery_slots = dquery_flat.reshape(E, SLOTS, local_width)
    gate_flat = to_slots(gate_one.reshape(-1, 1), attn_slot)
    dquery_back = jnp.einsum(
        "emh,edh->emd", dquery_slots, query_full, preferred_element_type=jnp.float32
    )
    dnormed_part_one = jnp.sum(
        from_slots(dquery_back.reshape(E * SLOTS, D), attn_slot).reshape(TOK, 2, D), axis=1
    )
    dnormed_part_one = dnormed_part_one + jnp.einsum(
        "kth,kdh->td", dkey_val, kv_full, preferred_element_type=jnp.float32
    )
    dnormed_one, dprob_one = lax.psum((dnormed_part_one, dprob_part_one), "narrow")
    dlogit_one = gate_back(prob_one, dprob_one, attn_mask)
    dnormed_one = dnormed_one + contract_cols(dlogit_one, router_one.astype(jnp.float32))
    gain_one_term = dnormed_one * stream_full * scale_one[:, None]
    gained_one = dnormed_one * gain_one.astype(jnp.float32)
    inner_one = jnp.sum(gained_one * stream_full, axis=-1)
    dstream = (
        dhidden
        + scale_one[:, None] * gained_one
        - stream_full * (scale_one**3 * inner_one / D)[:, None]
    )
    stream_grad = lax.dynamic_slice_in_dim(dstream, narrow_index * part_width, part_width, 1)
    query_grad = jnp.einsum(
        "emd,emh->edh", token_slots, dquery_slots, preferred_element_type=jnp.float32
    )
    weighted_grad = grad_slots.astype(jnp.float32) * gate_flat.reshape(E, SLOTS, 1)
    output_grad = split_product("emd,emh->edh", weighted_grad, context_slots)
    kv_grad = jnp.einsum("td,kth->kdh", normed_low, dkey_val, preferred_element_type=jnp.float32)
    gain_one_grad = jnp.sum(gain_one_term, axis=0)
    gain_two_grad = jnp.sum(gain_two_term, axis=0)
    router_one_grad = contract_rows(normed_one, dlogit_one)
    router_two_grad = contract_rows(normed_two, dlogit_two)
    grad_sums = (
        lax.psum_scatter(
            kv_grad.astype(jnp.bfloat16), "wide", scatter_dimension=1, tiled=True
        ).astype(jnp.float32),
        lax.psum_scatter(
            query_grad.astype(jnp.bfloat16), "wide", scatter_dimension=1, tiled=True
        ).astype(jnp.float32),
        lax.psum_scatter(
            output_grad.astype(jnp.bfloat16), "wide", scatter_dimension=1, tiled=True
        ).astype(jnp.float32),
        lax.psum_scatter(
            gain_one_grad.astype(jnp.bfloat16), "wide", scatter_dimension=0, tiled=True
        ).astype(jnp.float32),
        lax.psum_scatter(
            gain_two_grad.astype(jnp.bfloat16), "wide", scatter_dimension=0, tiled=True
        ).astype(jnp.float32),
        lax.psum_scatter(
            router_one_grad.astype(jnp.bfloat16), "wide", scatter_dimension=0, tiled=True
        ).astype(jnp.float32),
        lax.psum_scatter(
            router_two_grad.astype(jnp.bfloat16), "wide", scatter_dimension=0, tiled=True
        ).astype(jnp.float32),
    )
    kv_out, query_out, output_out = (grad_sums[0], grad_sums[1], grad_sums[2])
    gain_one_out, gain_two_out, router_one_out, router_two_out = (
        grad_sums[3],
        grad_sums[4],
        grad_sums[5],
        grad_sums[6],
    )
    return (
        layer_out,
        stream_grad,
        gain_one_out,
        router_one_out,
        kv_out,
        query_out,
        output_out,
        gain_two_out,
        router_two_out,
        up_grad[None],
        down_grad[None],
    )


def solution(mesh):
    in_specs = (
        P("wide", "narrow"),
        P("wide", "narrow"),
        P("wide"),
        P("wide", None),
        P(None, "wide", "narrow"),
        P(None, "wide", "narrow"),
        P(None, "wide", "narrow"),
        P("wide"),
        P("wide", None),
        P("wide", None, None, "narrow"),
        P("wide", "narrow", None),
        P("wide", None),
        P("wide", None),
        P("wide", None),
    )
    out_specs = (
        P("wide", "narrow"),
        P("wide", "narrow"),
        P("wide"),
        P("wide", None),
        P(None, "wide", "narrow"),
        P(None, "wide", "narrow"),
        P(None, "wide", "narrow"),
        P("wide"),
        P("wide", None),
        P("wide", None, None, "narrow"),
        P("wide", "narrow", None),
    )
    return jax.shard_map(local, mesh=mesh, in_specs=in_specs, out_specs=out_specs, check_vma=False)
```

profile of v0, /device:TPU:2, one launch (start us, length us, event | category | flops | bytes accessed | tf_op | source)
XLA Modules:
  0.0 1511.6 jit_solution(14368359595649202363)
XLA Ops:
  16.5 21.5 %all-gather.2 = bf16[8,1,256]{2,1,0:T(2,128)(2,1)S(1)} all-gather(bf16[1,1,256]{2,1,0:T(2,128)(2,1)S(1)} %reshape.670), channel_id=1, replica_groups=mesh['wide'=8,'narrow'=4] {'wide'}, dimensions={0}, use_global_device_ids=true | all-gather | bytes 4608 | tf_op jit(solution)/shard_map/all_gather | solution.py:163
  49.6 27.2 %all_gather.40 = bf16[2048,4]{0,1:T(4,128)(2,1)S(1)} all-gather(bf16[256,4]{0,1:T(4,128)(2,1)S(1)} %copy-done.84), channel_id=1, replica_groups=mesh['wide'=8,'narrow'=4] {'wide'}, dimensions={0}, use_global_device_ids=true | all-gather | bytes 18432 | tf_op jit(solution)/shard_map/all_gather | solution.py:165
  83.3 16.4 %all-gather.1 = s32[8,2,4]{2,1,0:T(2,128)S(1)} all-gather(s32[1,2,4]{2,1,0:T(2,128)S(1)} %add_bitcast_fusion.2), channel_id=2, replica_groups=mesh['wide'=8,'narrow'=4] {'wide'}, dimensions={0}, use_global_device_ids=true | all-gather | bytes 288 | tf_op jit(solution)/shard_map/all_gather | solution.py:21
  122.7 87.1 %all-gather.10.cloned.1.call-done = bf16[4,2048,512]{2,1,0:T(8,128)(2,1)} async-done(((bf16[4,256,512]{2,1,0:T(8,128)(2,1)}), bf16[4,2048,512]{2,1,0:T(8,128)(2,1)}) %all-gather.10.cloned.1.call-update) | async-done | bytes 8388624 | tf_op jit(solution)/shard_map/all_gather | solution.py:161
  229.3 105.4 %all-gather.12.cloned.1.call-done = bf16[4,2048,512]{2,1,0:T(8,128)(2,1)} async-done(((bf16[4,256,512]{2,1,0:T(8,128)(2,1)}), bf16[4,2048,512]{2,1,0:T(8,128)(2,1)}) %all-gather.12.cloned.1.call-update) | async-done | bytes 8388624 | tf_op jit(solution)/shard_map/all_gather | solution.py:162
  334.6 7.6 fusion.106
  362.8 17.7 %all-gather.3 = bf16[8,1,256]{2,1,0:T(2,128)(2,1)S(1)} all-gather(bf16[1,1,256]{2,1,0:T(2,128)(2,1)S(1)} %reshape.672), channel_id=1, replica_groups=mesh['wide'=8,'narrow'=4] {'wide'}, dimensions={0}, use_global_device_ids=true | all-gather | bytes 4608 | tf_op jit(solution)/shard_map/all_gather | solution.py:164
  381.1 13.1 all-reduce.7.cloned.1.call-done
  406.4 65.0 %all_to_all.20 = bf16[8,80,2048]{2,1,0:T(8,128)(2,1)S(1)} all-to-all(bf16[8,80,2048]{2,1,0:T(8,128)(2,1)S(1)} %bitcast.212), channel_id=1, replica_groups=mesh['wide'=8,'narrow'=4] {'wide'}, dimensions={0} | all-to-all | bytes 5242880 | tf_op jit(solution)/shard_map/all_to_all | solution.py:225
  471.4 7.7 fusion.2
  509.4 118.9 %all_gather.42 = bf16[2048,4]{0,1:T(4,128)(2,1)S(1)} all-gather(bf16[256,4]{0,1:T(4,128)(2,1)S(1)} %copy-done.85), channel_id=1, replica_groups=mesh['wide'=8,'narrow'=4] {'wide'}, dimensions={0}, use_global_device_ids=true | all-gather | bytes 18432 | tf_op jit(solution)/shard_map/all_gather | solution.py:166
  663.8 62.4 %all_to_all.21 = bf16[8,80,2048]{2,1,0:T(8,128)(2,1)S(1)} all-to-all(bf16[8,80,2048]{2,1,0:T(8,128)(2,1)S(1)} %bitcast.213), channel_id=1, replica_groups=mesh['wide'=8,'narrow'=4] {'wide'}, dimensions={0} | all-to-all | bytes 5242880 | tf_op jit(solution)/shard_map/all_to_all | solution.py:251
  733.0 9.8 fusion.4
  750.1 112.3 %all-to-all-done.3 = f32[8,80,2048]{2,1,0:T(8,128)} async-done(((f32[8,80,2048]{2,1,0:T(8,128)}), f32[8,80,2048]{2,1,0:T(8,128)}, u32[]{:S(2)}, u32[]{:S(2)}) %all-to-all-start.3) | async-done | bytes 5242912 | tf_op jit(solution)/shard_map/all_to_all | solution.py:271
  886.0 26.8 %all-reduce.9.cloned.1.call-done = f32[128,2048]{1,0:T(8,128)} async-done(((f32[128,2048]{1,0:T(8,128)}), f32[128,2048]{1,0:T(8,128)}) %all-reduce.9.cloned.1.call-update) | async-done | bytes 1048592 | tf_op jit(solution)/shard_map/psum | solution.py:277
  985.0 8.2 fusion.13
  993.2 11.5 add_convert_fusion
  1016.8 7.5 convolution_bitcast_fusion
  1024.3 44.9 %reduce-scatter.19.cloned.1.call-done = bf16[256,4]{1,0:T(8,128)(2,1)} async-done(((bf16[2048,4]{1,0:T(8,128)(2,1)}), bf16[256,4]{1,0:T(8,128)(2,1)}) %reduce-scatter.19.cloned.1.call-update) | async-done | bytes 2064
  1070.7 36.3 %all-reduce.11.cloned.1.call-done = f32[128,2048]{1,0:T(8,128)} async-done(((f32[128,2048]{1,0:T(8,128)}), f32[128,2048]{1,0:T(8,128)}) %all-reduce.11.cloned.1.call-update) | async-done | bytes 1048592 | tf_op jit(solution)/shard_map/psum | solution.py:349
  1110.0 22.2 %all-reduce.2 = (bf16[2048]{0:T(1024)(128)(2,1)S(1)}, bf16[2048]{0:T(1024)(128)(2,1)S(1)}) all-reduce(bf16[2048]{0:T(1024)(128)(2,1)S(1)} %get-tuple-element.82, bf16[2048]{0:T(1024)(128)(2,1)S(1)} %get-tuple-element.80), channel_id=4, replica_groups=mesh['wide'=8,'narrow'=4] {'wide'}, use_global_device_ids=true, to_apply=%region_52.54.clone | all-reduce | flops 4096 | bytes 16384
  1135.4 65.0 %reduce-scatter.13.cloned.1.call-done = bf16[2,256,512]{1,2,0:T(8,128)(2,1)} async-done(((bf16[2,2048,512]{1,2,0:T(8,128)(2,1)}), bf16[2,256,512]{1,2,0:T(8,128)(2,1)}) %reduce-scatter.13.cloned.1.call-update) | async-done | bytes 524304 | tf_op jit(solution)/shard_map/reduce_scatter | solution.py:372
  1202.6 148.9 %reduce-scatter.15.cloned.1.call-done = bf16[4,256,512]{2,1,0:T(8,128)(2,1)} async-done(((bf16[4,2048,512]{2,1,0:T(8,128)(2,1)}), bf16[4,256,512]{2,1,0:T(8,128)(2,1)}) %reduce-scatter.15.cloned.1.call-update) | async-done | bytes 1048592 | tf_op jit(solution)/shard_map/reduce_scatter | solution.py:375
  1354.5 147.1 %reduce-scatter.17.cloned.1.call-done = bf16[4,256,512]{2,1,0:T(8,128)(2,1)} async-done(((bf16[4,2048,512]{2,1,0:T(8,128)(2,1)}), bf16[4,256,512]{2,1,0:T(8,128)(2,1)}) %reduce-scatter.17.cloned.1.call-update) | async-done | bytes 1048592 | tf_op jit(solution)/shard_map/reduce_scatter | solution.py:378
  (413 shorter events, 304.9 us)
Async XLA Ops:
  7.2 477.4 %copy-start = (bf16[1,704,2048]{2,1,0:T(8,128)(2,1)S(1)}, bf16[1,704,2048]{2,1,0:T(8,128)(2,1)}, u32[]{:S(2)}) copy-start(bf16[1,704,2048]{2,1,0:T(8,128)(2,1)} %param.28) | copy-start | bytes 8650756
  7.2 108.4 %all-gather.8.cloned.1.call-start = ((), (), s32[]{:S(2)}) async-start(), calls=%async_computation.10 | async-start | bytes 4718592 | tf_op jit(solution)/shard_map/all_gather | solution.py:160
  8.0 201.8 %all-gather.10.cloned.1.call-start = ((), (), s32[]{:S(2)}) async-start(), calls=%async_computation.11 | async-start | bytes 9437184 | tf_op jit(solution)/shard_map/all_gather | solution.py:161
  8.7 325.9 %all-gather.12.cloned.1.call-start = ((), (), s32[]{:S(2)}) async-start(), calls=%async_computation.12 | async-start | bytes 9437184 | tf_op jit(solution)/shard_map/all_gather | solution.py:162
  9.5 384.8 %all-reduce.7.cloned.1.call-start = ((), (), s32[]{:S(2)}) async-start(), calls=%async_computation.13 | async-start | bytes 2097152 | tf_op jit(solution)/shard_map/psum | solution.py:212
  77.6 41.1 %copy-start.38 = (f32[128,2]{0,1:T(2,128)}, f32[128,2]{0,1:T(2,128)S(1)}, u32[]{:S(2)}) copy-start(f32[128,2]{0,1:T(2,128)S(1)} %select_reduce_fusion.4) | copy-start | bytes 3076
  222.0 120.3 %copy-start.48 = (f32[4,256]{1,0:T(4,128)}, f32[4,256]{1,0:T(4,128)S(1)}, u32[]{:S(2)}) copy-start(f32[4,256]{1,0:T(4,128)S(1)} %get-tuple-element.122) | copy-start | bytes 12292
  395.7 232.6 %copy-start.61 = (f32[128]{0:T(128)}, f32[128]{0:T(128)S(1)}, u32[]{:S(2)}) copy-start(f32[128]{0:T(128)S(1)} %add_rsqrt_fusion) | copy-start | bytes 1540
  490.3 141.1 %all-to-all-start.1 = ((f32[8,80,2048]{2,1,0:T(8,128)}), f32[8,80,2048]{2,1,0:T(8,128)}, u32[]{:S(2)}, u32[]{:S(2)}) async-start(f32[8,80,2048]{2,1,0:T(8,128)} %fusion.7), calls=%async_computation.1 | async-start | bytes 10485760 | tf_op jit(solution)/shard_map/all_to_all | solution.py:237
  508.6 127.5 %copy-start.79 = (pred[256]{0:T(512)(128)(4,1)}, pred[256]{0:T(512)(128)(4,1)S(1)}, u32[]{:S(2)}) copy-start(pred[256]{0:T(512)(128)(4,1)S(1)} %get-tuple-element.109) | copy-start | bytes 772
  508.6 132.8 %copy-start.74 = (pred[256]{0:T(512)(128)(4,1)}, pred[256]{0:T(512)(128)(4,1)S(1)}, u32[]{:S(2)}) copy-start(pred[256]{0:T(512)(128)(4,1)S(1)} %get-tuple-element.107) | copy-start | bytes 772
  663.8 62.5 %copy-start.20 = (f32[640,2,704]{0,2,1:T(8,128)S(1)}, f32[640,2,704]{0,2,1:T(8,128)}, u32[]{:S(2)}) copy-start(f32[640,2,704]{0,2,1:T(8,128)} %copy-done.19) | copy-start | bytes 10813444
  742.8 119.6 %all-to-all-start.3 = ((f32[8,80,2048]{2,1,0:T(8,128)}), f32[8,80,2048]{2,1,0:T(8,128)}, u32[]{:S(2)}, u32[]{:S(2)}) async-start(f32[8,80,2048]{2,1,0:T(8,128)} %fusion.4), calls=%async_computation.4 | async-start | bytes 10485760 | tf_op jit(solution)/shard_map/all_to_all | solution.py:271
  747.6 165.2 %all-reduce.9.cloned.1.call-start = ((), (), s32[]{:S(2)}) async-start(), calls=%async_computation.15 | async-start | bytes 2097152 | tf_op jit(solution)/shard_map/psum | solution.py:277
  877.7 128.9 %reduce-scatter.21.cloned.1.call-start = ((), (), s32[]{:S(2)}) async-start(), calls=%async_computation.21 | async-start | bytes 589824
  879.8 128.3 %reduce-scatter.11.cloned.1.call-start = ((), (), s32[]{:S(2)}) async-start(), calls=%async_computation.14 | async-start | bytes 655360 | tf_op jit(solution)/shard_map/reduce_scatter | solution.py:242
  885.5 183.7 %reduce-scatter.19.cloned.1.call-start = ((), (), s32[]{:S(2)}) async-start(), calls=%async_computation.20 | async-start | bytes 589824
  967.3 139.7 %all-reduce.11.cloned.1.call-start = ((), (), s32[]{:S(2)}) async-start(), calls=%async_computation.16 | async-start | bytes 2097152 | tf_op jit(solution)/shard_map/psum | solution.py:349
  972.1 228.3 %reduce-scatter.13.cloned.1.call-start = ((), (), s32[]{:S(2)}) async-start(), calls=%async_computation.17 | async-start | bytes 4718592 | tf_op jit(solution)/shard_map/reduce_scatter | solution.py:372
  975.5 376.0 %reduce-scatter.15.cloned.1.call-start = ((), (), s32[]{:S(2)}) async-start(), calls=%async_computation.18 | async-start | bytes 9437184 | tf_op jit(solution)/shard_map/reduce_scatter | solution.py:375
  982.5 519.1 %reduce-scatter.17.cloned.1.call-start = ((), (), s32[]{:S(2)}) async-start(), calls=%async_computation.19 | async-start | bytes 9437184 | tf_op jit(solution)/shard_map/reduce_scatter | solution.py:378
  1016.8 90.2 %copy-start.37 = (bf16[2048,4]{0,1:T(4,128)(2,1)S(1)}, bf16[2048,4]{0,1:T(4,128)(2,1)}, u32[]{:S(2)}) copy-start(bf16[2048,4]{0,1:T(4,128)(2,1)} %copy-done.36) | copy-start | bytes 49156
  1024.3 109.2 %copy-start.89 = (f32[128]{0:T(128)S(1)}, f32[128]{0:T(128)}, u32[]{:S(2)}) copy-start(f32[128]{0:T(128)} %copy-done.88) | copy-start | bytes 1540
  1351.5 152.9 %copy-start.1 = (bf16[1,704,2048]{2,1,0:T(8,128)(2,1)S(1)}, bf16[1,704,2048]{2,1,0:T(8,128)(2,1)}, u32[]{:S(2)}) copy-start(bf16[1,704,2048]{2,1,0:T(8,128)(2,1)} %param.28) | copy-start | bytes 8650756
  (85 other events, 559.0 us)
Sparse Core Ops, SparseCore 0:
  10.2 74.3 all-gather.7
  86.8 122.9 all-gather.9
  212.0 122.6 all-gather.11
  360.2 34.0 all-reduce.6
  877.8 34.8 all-reduce.8
  915.9 63.5 reduce-scatter.20
  982.0 19.4 reduce-scatter.10
  1005.4 63.7 reduce-scatter.18
  1072.1 34.7 all-reduce.10
  1110.5 89.8 reduce-scatter.12
  1204.0 147.4 reduce-scatter.14
  1355.0 146.5 reduce-scatter.16
where the time goes:
time: 1520 us; the launch traced here: 1510 us
  waiting for transfers between devices  789 us (52%)
  blocking collectives  376 us (25%)
  local copies, waits for them, and re-layouts  120 us (8%)
  matrix products  116 us (8%)
  other arithmetic  83.7 us (6%)
  between operations  16.4 us (1%)
    reduce_scatter x1, waiting for transfers between devices, local(): lax.psum_scatter(query_grad.astype(jnp.bfloat16), 'wide', scatter_dimensi...  149 us
    reduce_scatter x1, waiting for transfers between devices, local(): lax.psum_scatter(output_grad.astype(jnp.bfloat16), 'wide', scatter_dimens...  147 us
    all_gather x1, blocking collectives, local(): lax.all_gather(mlp_router, 'wide', axis=0, tiled=True)  119 us
    all_to_all x1, waiting for transfers between devices, local(): lax.all_to_all(drows_back.reshape(wide_count, SLOTS, D), 'wide', split_ax...  112 us
    all_gather x1, waiting for transfers between devices, local(): lax.all_gather(output_proj, 'wide', axis=1, tiled=True)  105 us
    all_gather x1, waiting for transfers between devices, local(): lax.all_gather(query_proj, 'wide', axis=1, tiled=True)  87.1 us
    reduce_scatter x1, waiting for transfers between devices, local(): lax.psum_scatter(kv_grad.astype(jnp.bfloat16), 'wide', scatter_dimension=...  65 us
    all_to_all x1, blocking collectives, local(): lax.all_to_all(send_rows, 'wide', split_axis=0, concat_axis=0, tiled=True)  65 us
  transfers between devices with their start and end apart: 14, of which 10 were waited for; matrix products, arithmetic and copies ran while one was open for 13% of the time, Pallas kernels for 0%

commit v1 on v0

v1 whole, which is shorter than its diff:
```python
import jax
import jax.numpy as jnp
from jax import lax
from jax.sharding import PartitionSpec as P

HS = 128
E = 4
TOPK = 2
TOK = 128
SLOTS = 80

EPSILON = 1e-05
NEGATIVE = -1000000000.0
PRECISE = lax.Precision.HIGHEST
F32 = jnp.float32
BF16 = jnp.bfloat16


def dot(left, right, contract, precision=None):
    return lax.dot_general(
        left, right, ((contract[0], contract[1]), ((), ())), precision=precision, preferred_element_type=F32
    )


def xor_shuffle(values, amount):
    count, bit = values.shape[0], 1
    while bit < count:
        split = values.reshape((count // (2 * bit), 2, bit) + values.shape[1:])
        flipped = split[:, ::-1].reshape(values.shape)
        values = jnp.where((amount & bit) != 0, flipped, values)
        bit *= 2
    return values


def local(
    stream,
    out_grad,
    attn_gain,
    attn_router,
    key_value,
    query_proj,
    output_proj,
    mlp_gain,
    mlp_router,
    expert_in,
    expert_down,
    attn_routes,
    mlp_routes,
    doc_lengths,
):
    wide_count = lax.axis_size("wide")
    narrow_count = lax.axis_size("narrow")
    subs = wide_count // E
    wide = lax.axis_index("wide")
    narrow = lax.axis_index("narrow")
    plane, sub = wide // subs, wide % subs
    capacity = 9 * TOK * wide_count * TOPK // (8 * E)
    slice_width = stream.shape[1]
    shard_rows = attn_gain.shape[0]
    width = slice_width * narrow_count
    local_width = key_value.shape[2]
    head_count = local_width // HS
    hidden_units = expert_down.shape[1]
    score_scale = HS ** (-0.5)

    def by_plane(values, k):
        return lax.ppermute(values, "wide", [(i, i ^ (k * subs)) for i in range(wide_count)])

    def by_sub(values, k):
        return lax.ppermute(values, "wide", [(i, i ^ k) for i in range(wide_count)])

    def by_narrow(values, k):
        return lax.ppermute(values, "narrow", [(i, i ^ k) for i in range(narrow_count)])

    def swap(values):
        pairs = []
        for w in range(wide_count):
            for n in range(narrow_count):
                z, y = w // subs, w % subs
                pairs.append((w * narrow_count + n, (n * subs + y) * narrow_count + z))
        return lax.ppermute(values, ("wide", "narrow"), pairs)

    def gather_planes(values):
        return [values] + [by_plane(values, k) for k in range(1, E)]

    def exchange_planes(parts):
        return [parts[0]] + [by_plane(parts[k], k) for k in range(1, E)]

    def gather_subs(values):
        parts, bit = [values], 1
        while bit < subs:
            parts = parts + [by_sub(one, bit) for one in parts]
            bit *= 2
        return parts

    def reduce_subs(parts):
        bit = subs // 2
        while bit >= 1:
            parts = [parts[j] + by_sub(parts[j + bit].astype(BF16), bit).astype(F32) for j in range(bit)]
            bit //= 2
        return parts[0]

    def gather_narrow(values):
        two = jnp.stack([values, by_narrow(values, 2)])
        one = by_narrow(two, 1)
        return jnp.stack([two[0], one[0], two[1], one[1]])

    def reduce_narrow(parts):
        low = parts.astype(BF16)
        two = jnp.stack([parts[0], parts[1]]) + by_narrow(low[2:4], 2).astype(F32)
        return two[0] + by_narrow(two[1].astype(BF16), 1).astype(F32)

    def sum_narrow(values):
        values = values + by_narrow(values, 2)
        return values + by_narrow(values, 1)

    def sum_planes(values):
        values = values + by_plane(values, 1)
        return values + by_plane(values, 2)

    def sum_subs(values):
        bit = 1
        while bit < subs:
            values = values + by_sub(values, bit)
            bit *= 2
        return values

    own_rows = jnp.concatenate(
        [attn_gain[None, :], attn_router.T, mlp_gain[None, :], mlp_router.T], axis=0
    )
    own_routes = jnp.concatenate([attn_routes.T, mlp_routes.T], axis=0)
    route_rows = own_routes.astype(BF16).reshape(-1, shard_rows)
    packed = jnp.concatenate([own_rows, route_rows], axis=0)
    used = packed.shape[0]
    packed = jnp.pad(packed, ((0, -used % 16), (0, 0)))
    parts = gather_subs(packed)
    by_k = [gather_planes(one) for one in parts]
    table = jnp.stack([by_k[j][k] for k in range(E) for j in range(subs)])
    table = xor_shuffle(table, wide)
    gain_one = table[:, 0].reshape(width).astype(F32)
    router_one = table[:, 1:5].swapaxes(0, 1).reshape(E, width)
    gain_two = table[:, 5].reshape(width).astype(F32)
    router_two = table[:, 6:10].swapaxes(0, 1).reshape(E, width)
    routes = table[:, 10:used].reshape(wide_count, 4, TOK).astype(jnp.int32)

    experts = jnp.arange(E, dtype=jnp.int32)
    hot = (routes[:, :, :, None] == experts).astype(F32)
    hot = hot.reshape(wide_count, 2, 2, TOK, E)
    both = jnp.sum(hot, axis=2).swapaxes(0, 1)
    earlier = (jnp.arange(TOK)[:, None] > jnp.arange(TOK)[None, :]).astype(BF16)
    rank = jnp.einsum("ts,awse->awte", earlier, both.astype(BF16), preferred_element_type=F32)
    counts = jnp.sum(both, axis=2)
    blocks = jnp.arange(wide_count)
    prefix = jnp.sum(
        jnp.where((blocks[:, None] > blocks[None, :])[None, :, :, None], counts[:, None], 0.0), axis=2
    )
    kept = both * ((prefix[:, :, None, :] + rank) < capacity).astype(F32)

    def pick(values, index):
        return lax.dynamic_index_in_dim(values, index, 0, False)

    turned = narrow * subs + sub
    hot_one = pick(hot[:, 0], wide)
    keep_one = jnp.sum(hot_one * pick(kept[0], wide)[None], axis=-1)
    hot_two = pick(hot[:, 1], turned)
    kept_two = pick(kept[1], turned)
    rank_two = pick(rank[1], turned)
    keep_two = jnp.sum(hot_two * kept_two[None], axis=-1)
    slots = jnp.arange(SLOTS, dtype=F32)
    rank_k = xor_shuffle(rank_two.T, plane)
    kept_k = xor_shuffle(kept_two.T, plane)
    select = jnp.where(
        (rank_k[:, None, :] == slots[None, :, None]) & (kept_k[:, None, :] > 0), 1.0, 0.0
    ).astype(BF16)
    own_expert = (experts == plane).astype(F32)
    rank_m = xor_shuffle(jnp.sum(rank[1] * own_expert, axis=-1), turned)
    kept_m = xor_shuffle(jnp.sum(kept[1] * own_expert, axis=-1), turned)
    both_m = xor_shuffle(both[1], turned)
    select_m = jnp.where(
        (rank_m[:, None, :] == slots[None, :, None]) & (kept_m[:, None, :] > 0), 1.0, 0.0
    ).astype(BF16)
    row_hot = jnp.einsum("wst,wte->wse", select_m, both_m.astype(BF16), preferred_element_type=F32)
    row_hot = row_hot.reshape(-1, E)

    hot_k = hot[:, 0].reshape(E, subs, 2, TOK, E)
    hot_k = lax.dynamic_index_in_dim(hot_k, sub, 1, False)
    hot_k = xor_shuffle(hot_k, plane)

    kv_parts = gather_subs(key_value)
    query_parts = gather_subs(query_proj)
    home_stream = stream.astype(F32)
    turned_stream = swap(stream)
    turned_grad = swap(out_grad)

    def widen(values):
        everyone = xor_shuffle(gather_narrow(values), narrow ^ plane)
        pieces = everyone.reshape(E, TOK, subs, shard_rows).transpose(2, 0, 1, 3)
        return xor_shuffle(pieces, sub)

    def own_slice(vector, place):
        return lax.dynamic_slice_in_dim(vector, place * slice_width, slice_width, vector.ndim - 1)

    gain_one_plane = own_slice(gain_one, plane)
    gain_two_plane = own_slice(gain_two, plane)
    router_two_plane = own_slice(router_two, plane).astype(F32)
    gain_one_home = own_slice(gain_one, narrow)
    router_one_home = own_slice(router_one, narrow).astype(F32)

    wide_stream = widen(turned_stream)
    gain_pieces = xor_shuffle(gain_one_plane.reshape(subs, shard_rows), sub)
    gained = (wide_stream.astype(F32) * gain_pieces[:, None, None, :]).astype(BF16)
    gained = gained.reshape(subs, E * TOK, shard_rows)

    def project(rows, weights):
        total = None
        for j in range(subs):
            one = jnp.einsum("td,adc->atc", rows[j], weights[j], preferred_element_type=F32)
            total = one if total is None else total + one
        return total

    def choose(every):
        shaped = every.reshape(E, E, TOK, -1)
        pairs = []
        for k2 in range(TOPK):
            mask = hot_k[:, k2]
            total = jnp.where(mask[:, :, 0:1] > 0, shaped[0], 0.0)
            for e in range(1, E):
                total = jnp.where(mask[:, :, e : e + 1] > 0, shaped[e], total)
            pairs.append(total)
        return jnp.stack(pairs, axis=1)

    def scatter_planes(partial):
        got = exchange_planes([None] + [partial[k].astype(BF16) for k in range(1, E)])
        total = partial[0]
        for k in range(1, E):
            total = total + got[k].astype(F32)
        return total

    kv_partial = project(gained, kv_parts).reshape(2, E, TOK, local_width).swapaxes(0, 1)
    key_val = scatter_planes(kv_partial)
    query_partial = choose(project(gained, query_parts))
    query_raw = scatter_planes(query_partial)

    gained_home = home_stream * gain_one_home
    stats_one = jnp.concatenate(
        [
            jnp.sum(home_stream * home_stream, axis=-1)[None],
            dot(router_one_home, gained_home, ((1,), (1,)), PRECISE),
        ],
        axis=0,
    )
    stats_one = sum_narrow(stats_one)
    scale_one = lax.rsqrt(stats_one[0] / width + EPSILON)
    logits_one = (stats_one[1:] * scale_one).T

    def gates(logits, hots):
        picked = jnp.sum(hots * logits[None], axis=-1)
        gap = picked[0] - picked[1]
        return jnp.stack([jax.nn.sigmoid(gap), jax.nn.sigmoid(-gap)])

    prob_one = gates(logits_one, hot_one)
    gate_one = prob_one * keep_one
    key_val = (key_val * scale_one[None, :, None]).astype(BF16)
    query = (query_raw * scale_one[None, :, None]).astype(BF16)

    doc_ends = jnp.cumsum(doc_lengths[0])
    positions = jnp.arange(TOK, dtype=jnp.int32)
    member = jnp.sum((positions[:, None] >= doc_ends[None, :]).astype(jnp.int32), axis=1)
    allowed = (member[:, None] == member[None, :]) & (positions[None, :] <= positions[:, None])
    allowed = jnp.concatenate([allowed, allowed], axis=0)
    query_rows = query.reshape(TOPK * TOK, head_count, HS)
    key_rows = key_val[0].reshape(TOK, head_count, HS)
    value_rows = key_val[1].reshape(TOK, head_count, HS)
    scores = (
        jnp.einsum("rhc,jhc->hrj", query_rows, key_rows, preferred_element_type=F32) * score_scale
    )
    scores = jnp.where(allowed[None], scores, NEGATIVE)
    exp_scores = jnp.exp(scores - jnp.max(scores, axis=-1, keepdims=True))
    probs = exp_scores / jnp.sum(exp_scores, axis=-1, keepdims=True)
    probs_low = probs.astype(BF16)
    context = jnp.einsum("hrj,jhc->rhc", probs_low, value_rows, preferred_element_type=F32).astype(BF16)
    context = context.reshape(TOPK, TOK, local_width)
    gated = (context.astype(F32) * gate_one[:, :, None]).astype(BF16)

    out_parts = gather_subs(output_proj)

    def spread(pairs):
        result = []
        for e in range(E):
            first = jnp.where(hot_k[:, 0, :, e : e + 1] > 0, pairs[:, 0], jnp.zeros((), BF16))
            one = jnp.where(hot_k[:, 1, :, e : e + 1] > 0, pairs[:, 1], first)
            result.append(one.reshape(E * TOK, -1))
        return result

    def back(rows, weights):
        total = None
        for a in range(len(rows)):
            one = dot(rows[a], weights[a], ((1,), (1,)))
            total = one if total is None else total + one
        return total

    def to_turned(pieces):
        by_block = jnp.stack(pieces).reshape(subs, E, TOK, shard_rows).transpose(1, 0, 2, 3)
        by_block = xor_shuffle(by_block, narrow ^ plane)
        total = xor_shuffle(reduce_narrow(by_block), sub)
        return total.transpose(1, 0, 2).reshape(TOK, slice_width)

    mixed = spread(jnp.stack(gather_planes(gated)))
    attention = to_turned([back(mixed, out_parts[j]) for j in range(subs)])
    hidden = turned_stream.astype(F32) + attention

    def dispatch(rows):
        picked = jnp.einsum("kst,td->ksd", select, rows, preferred_element_type=F32).astype(BF16)
        got = xor_shuffle(jnp.stack(exchange_planes([picked[k] for k in range(E)])), plane)
        full = got.swapaxes(0, 1).reshape(SLOTS, width)
        full = jnp.stack(gather_subs(full))
        return gather_narrow(full).reshape(-1, width)

    grad_rows = dispatch(turned_grad)
    weight_in = expert_in[0]
    weight_down = expert_down[0]
    dact_raw = dot(grad_rows, weight_down, ((1,), (1,)))

    expert_rows = dispatch((hidden * gain_two_plane).astype(BF16))
    stats_two = jnp.concatenate(
        [
            jnp.sum(hidden * hidden, axis=-1)[None],
            dot(router_two_plane, hidden * gain_two_plane, ((1,), (1,)), PRECISE),
        ],
        axis=0,
    )
    stats_two = sum_planes(stats_two)
    scale_two = lax.rsqrt(stats_two[0] / width + EPSILON)
    logits_two = (stats_two[1:] * scale_two).T
    prob_two = gates(logits_two, hot_two)

    rows_float = expert_rows.astype(F32) / gain_two
    row_scale = lax.rsqrt(jnp.sum(rows_float * rows_float, axis=-1, keepdims=True) / width + EPSILON)
    row_logits = dot(expert_rows, router_two, ((1,), (1,)))
    row_gap = jnp.sum((2.0 * own_expert[None, :] - row_hot) * row_logits, axis=-1, keepdims=True)
    row_gate = jax.nn.sigmoid(row_gap * row_scale)
    gate_up = jnp.einsum("rd,dkf->krf", expert_rows, weight_in, preferred_element_type=F32)
    gate_pre = gate_up[0] * row_scale
    up_pre = gate_up[1] * row_scale
    gate_sig = jax.nn.sigmoid(gate_pre)
    silu_gate = gate_pre * gate_sig
    activation = (silu_gate * up_pre).astype(BF16)
    dactiv = dact_raw * row_gate
    dgate_pre = (dactiv * up_pre * gate_sig * (1.0 + gate_pre * (1.0 - gate_sig))).astype(BF16)
    dup_pre = (dactiv * silu_gate).astype(BF16)
    dprob_rows = jnp.sum(activation.astype(F32) * dact_raw, axis=-1)
    inner_rows = jnp.sum(dgate_pre.astype(F32) * gate_pre + dup_pre.astype(F32) * up_pre, axis=-1)
    drows = jnp.einsum(
        "krf,dkf->rd", jnp.stack([dgate_pre, dup_pre]), weight_in, preferred_element_type=F32
    )
    lanes = jnp.arange(128)
    row_stats = jnp.where(
        lanes[None, :] == 0, dprob_rows[:, None], jnp.where(lanes[None, :] == 1, inner_rows[:, None], 0.0)
    )

    def give_back(rows):
        shaped = rows.reshape(narrow_count, subs, SLOTS, -1)
        low = shaped.astype(BF16)
        got = by_narrow(jnp.stack([low[1], low[3]]), 1)
        two = jnp.stack([shaped[0], shaped[2]]) + got.astype(F32)
        one = two[0] + by_narrow(two[1].astype(BF16), 2).astype(F32)
        return reduce_subs([one[j] for j in range(subs)])

    def from_planes(rows, extra=None):
        pieces = rows.astype(BF16).reshape(SLOTS, E, slice_width).swapaxes(0, 1)
        pieces = xor_shuffle(pieces, plane)
        if extra is not None:
            more = jnp.broadcast_to(extra.astype(BF16)[None], (E,) + extra.shape)
            pieces = jnp.concatenate([pieces, more], axis=-1)
        return jnp.stack(exchange_planes([pieces[k] for k in range(E)]))

    returned = give_back(jnp.concatenate([drows, row_stats], axis=1))
    returned = from_planes(returned[:, :width], returned[:, width:])
    combined = jnp.einsum("kst,ksd->ktd", select, returned, preferred_element_type=F32)
    per_expert = xor_shuffle(combined[:, :, slice_width : slice_width + 2], plane)
    dprob_two = keep_two * jnp.sum(hot_two * per_expert[:, :, 0].T[None], axis=-1)
    inner_two = jnp.sum(per_expert[:, :, 1], axis=0)
    dnormed_two = jnp.sum(combined[:, :, :slice_width], axis=0)

    def gate_back(prob, dprob, hots):
        dselect = prob * (dprob - jnp.sum(prob * dprob, axis=0, keepdims=True))
        return jnp.sum(hots * dselect[:, :, None], axis=0)

    dlogit_two = gate_back(prob_two, dprob_two, hot_two)
    dnormed_two = dnormed_two + dot(dlogit_two, router_two_plane, ((1,), (0,)), PRECISE)
    inner_two = inner_two + jnp.sum(dlogit_two * logits_two, axis=-1)
    dhidden = (
        turned_grad.astype(F32)
        + scale_two[:, None] * (dnormed_two * gain_two_plane)
        - hidden * (scale_two * scale_two * inner_two / width)[:, None]
    )
    scaled_hidden = hidden * scale_two[:, None]
    mlp_terms = jnp.concatenate(
        [
            jnp.sum(dnormed_two * scaled_hidden, axis=0)[None],
            dot(dlogit_two, scaled_hidden * gain_two_plane, ((0,), (0,)), PRECISE),
        ],
        axis=0,
    )

    wide_grad = widen(dhidden.astype(BF16)).reshape(subs, E * TOK, shard_rows)
    dcontext_raw = scatter_planes(choose(project(wide_grad, out_parts)))
    output_grad = reduce_subs(
        [jnp.stack([dot(wide_grad[j], mixed[e], ((0,), (0,))) for e in range(E)]) for j in range(subs)]
    )
    dcontext = (dcontext_raw * gate_one[:, :, None]).astype(BF16)
    dcontext_rows = dcontext.reshape(TOPK * TOK, head_count, HS)
    dweights = jnp.einsum("rhc,jhc->hrj", dcontext_rows, value_rows, preferred_element_type=F32)
    dscores = (probs * (dweights - jnp.sum(probs * dweights, axis=-1, keepdims=True))).astype(BF16)
    dquery = (
        jnp.einsum("hrj,jhc->rhc", dscores, key_rows, preferred_element_type=F32) * score_scale
    ).reshape(TOPK, TOK, local_width)
    dkeys = (
        jnp.einsum("hrj,rhc->jhc", dscores, query_rows, preferred_element_type=F32) * score_scale
    ).reshape(TOK, local_width)
    dvalues = jnp.einsum(
        "hrj,rhc->jhc", probs_low, dcontext_rows, preferred_element_type=F32
    ).reshape(TOK, local_width)
    dkey_val = jnp.stack([dkeys, dvalues])
    home_sums = jnp.concatenate(
        [
            jnp.sum(context.astype(F32) * dcontext_raw, axis=-1),
            (
                jnp.sum(dquery * query.astype(F32), axis=(0, 2))
                + jnp.sum(dkey_val * key_val.astype(F32), axis=(0, 2))
            )[None],
        ],
        axis=0,
    )
    home_sums = sum_narrow(home_sums)
    dprob_one = keep_one * home_sums[:2]
    dlogit_one = gate_back(prob_one, dprob_one, hot_one)
    inner_one = home_sums[2] + jnp.sum(dlogit_one * logits_one, axis=-1)
    dlogit_scaled = dlogit_one * scale_one[:, None]

    dkv_low = (dkey_val * scale_one[None, :, None]).astype(BF16)
    dkv_all = jnp.stack(gather_planes(dkv_low), axis=1).reshape(2, E * TOK, local_width)
    dlogit_low = dlogit_scaled.T.astype(BF16)
    dlogit_rest = (dlogit_scaled.T - dlogit_low.astype(F32)).astype(BF16)
    dlogit_rows = jnp.concatenate([dlogit_low.reshape(1, -1), dlogit_rest.reshape(1, -1)], axis=0)
    dquery_low = (dquery * scale_one[None, :, None]).astype(BF16).reshape(TOPK * TOK, local_width)
    dquery_sent = jnp.concatenate([dquery_low, jnp.pad(dlogit_rows, ((0, 14), (0, 0)))], axis=0)
    dquery_all = jnp.stack(gather_planes(dquery_sent))
    dlogit_all = jnp.sum(dquery_all[:, TOPK * TOK : TOPK * TOK + 2].astype(F32), axis=1)
    dlogit_all = dlogit_all.reshape(E, E, TOK).swapaxes(1, 2).reshape(E * TOK, E)
    dquery_all = dquery_all[:, : TOPK * TOK].reshape(E, TOPK, TOK, local_width)
    dmixed = spread(dquery_all)

    kv_grad = reduce_subs(
        [jnp.stack([dot(gained[j], dkv_all[a], ((0,), (0,))) for a in range(2)]) for j in range(subs)]
    )
    query_grad = reduce_subs(
        [jnp.stack([dot(gained[j], dmixed[e], ((0,), (0,))) for e in range(E)]) for j in range(subs)]
    )
    dnormed_one = to_turned(
        [
            back([dkv_all[0], dkv_all[1]], kv_parts[j]) + back(dmixed, query_parts[j])
            for j in range(subs)
        ]
    )
    turned_out = dhidden + dnormed_one * gain_one_plane
    home_out = swap(turned_out.astype(BF16)).astype(F32)
    stream_grad = (
        home_out
        + gain_one_home * dot(dlogit_scaled, router_one_home, ((1,), (0,)), PRECISE)
        - home_stream * (scale_one * scale_one * inner_one / width)[:, None]
    )

    gain_term = jnp.sum(dnormed_one * turned_stream.astype(F32), axis=0)
    small = jnp.concatenate([mlp_terms, gain_term[None]], axis=0)
    small = sum_narrow(small)
    gained_plane = xor_shuffle(gained, sub).transpose(1, 0, 2).reshape(E * TOK, slice_width)
    router_term = dot(dlogit_all, gained_plane.astype(F32), ((0,), (0,)), PRECISE)
    small = sum_subs(jnp.concatenate([small, router_term], axis=0))
    mine = lax.dynamic_slice_in_dim(small, sub * shard_rows, shard_rows, 1)
    router_one_grad = mine[6:10]
    gain_one_grad = mine[5] + jnp.sum(
        router_one_grad * attn_router.T.astype(F32), axis=0
    ) / attn_gain.astype(F32)

    expert_out = dot(activation, weight_down, ((1,), (0,))) * row_gate
    mixture = from_planes(give_back(expert_out))
    mixture = jnp.einsum("kst,ksd->td", select, mixture, preferred_element_type=F32)
    layer_out = swap((hidden + mixture).astype(BF16)).astype(F32)
    gated_act = (activation.astype(F32) * row_gate).astype(BF16)
    down_grad = dot(gated_act, grad_rows, ((0,), (0,)))
    dboth = jnp.stack(
        [
            (dgate_pre.astype(F32) * row_scale).astype(BF16),
            (dup_pre.astype(F32) * row_scale).astype(BF16),
        ],
        axis=1,
    )
    up_grad = jnp.einsum("rd,rkf->dkf", expert_rows, dboth, preferred_element_type=F32)

    return (
        layer_out,
        stream_grad,
        gain_one_grad,
        router_one_grad.T,
        kv_grad,
        query_grad,
        output_grad,
        mine[0],
        mine[1:5].T,
        up_grad[None],
        down_grad[None],
    )


def solution(mesh):
    in_specs = (
        P("wide", "narrow"),
        P("wide", "narrow"),
        P("wide"),
        P("wide", None),
        P(None, "wide", "narrow"),
        P(None, "wide", "narrow"),
        P(None, "wide", "narrow"),
        P("wide"),
        P("wide", None),
        P("wide", None, None, "narrow"),
        P("wide", "narrow", None),
        P("wide", None),
        P("wide", None),
        P("wide", None),
    )
    out_specs = (
        P("wide", "narrow"),
        P("wide", "narrow"),
        P("wide"),
        P("wide", None),
        P(None, "wide", "narrow"),
        P(None, "wide", "narrow"),
        P(None, "wide", "narrow"),
        P("wide"),
        P("wide", None),
        P("wide", None, None, "narrow"),
        P("wide", "narrow", None),
    )
    return jax.shard_map(local, mesh=mesh, in_specs=in_specs, out_specs=out_specs, check_vma=False)
```

time: 1520 us -> 570 us (0.38)
  the two profiles are of different devices: /device:TPU:2 before, /device:TPU:0 now
where the time goes in v1:
time: 570 us; the launch traced here: 558 us
  waiting for transfers between devices  181 us (32%)
  starting transfers between devices  111 us (19%)
  matrix products  97.1 us (17%)
  other arithmetic  86.1 us (15%)
  local copies, waits for them, and re-layouts  78.4 us (14%)
    ppermute x38, waiting for transfers between devices, by_plane(): lax.ppermute(values, 'wide', [(i, i ^ k * subs) for i in range(wide_count)])  96.7 us
    ppermute x38, starting transfers between devices, by_plane(): lax.ppermute(values, 'wide', [(i, i ^ k * subs) for i in range(wide_count)])  77.9 us
    ppermute x22, waiting for transfers between devices, by_narrow(): lax.ppermute(values, 'narrow', [(i, i ^ k) for i in range(narrow_count)])  57.4 us
    dot_general x50, matrix products, dot(): lax.dot_general(left, right, ((contract[0], contract[1]), ((), ())), prec...  55.9 us
    ppermute x12, waiting for transfers between devices, by_sub(): return lax.ppermute(values, 'wide', [(i, i ^ k) for i in range(wide_count)])  26.6 us
    rev x37, local copies, waits for them, and re-layouts, xor_shuffle(): flipped = split[:, ::-1].reshape(values.shape)  19.2 us
    select_n x34, other arithmetic, xor_shuffle(): values = jnp.where(amount & bit != 0, flipped, values)  17.5 us
    ppermute x12, starting transfers between devices, by_sub(): return lax.ppermute(values, 'wide', [(i, i ^ k) for i in range(wide_count)])  15.9 us
  transfers between devices with their start and end apart: 76, of which 31 were waited for; matrix products, arithmetic and copies ran while one was open for 36% of the time, Pallas kernels for 0%

profile of v1, /device:TPU:0, one launch (start us, length us, event | category | flops | bytes accessed | tf_op | source)
XLA Modules:
  0.0 558.4 jit_solution(9937449551800823796)
XLA Ops:
  24.6 4.2 collective-permute-start.5
  32.6 4.5 collective-permute-start.7
  52.8 5.7 %collective-permute-done.8 = bf16[128,512]{1,0:T(8,128)(2,1)S(1)} collective-permute-done((bf16[128,512]{1,0:T(8,128)(2,1)S(1)}, bf16[128,512]{1,0:T(8,128)(2,1)S(1)}, u32[]{:S(2)}, u32[]{:S(2)}) %collective-permute-start.8) | collective-permute-done | bytes 131104 | tf_op jit(solution)/shard_map/ppermute | solution.py:73
  91.6 10.4 %collective-permute-start.17 = (bf16[2,128,512]{2,1,0:T(8,128)(2,1)S(1)}, bf16[2,128,512]{2,1,0:T(8,128)(2,1)S(1)}, u32[]{:S(2)}, u32[]{:S(2)}) collective-permute-start(bf16[2,128,512]{2,1,0:T(8,128)(2,1)S(1)} %get-tuple-element.73), channel_id=1, source_target_pairs={{0,8},{4,12},{8,0},{12,4},{16,24},{20,28},{24,16},{28,20},{1,9},{5... | collective-permute-start | bytes 786440 | tf_op jit(solution)/shard_map/ppermute | solution.py:67
  104.1 14.3 %collective-permute-done.12 = bf16[2,128,512]{2,1,0:T(8,128)(2,1)S(1)} collective-permute-done((bf16[2,128,512]{2,1,0:T(8,128)(2,1)S(1)}, bf16[2,128,512]{2,1,0:T(8,128)(2,1)S(1)}, u32[]{:S(2)}, u32[]{:S(2)}) %collective-permute-start.12) | collective-permute-done | bytes 262176 | tf_op jit(solution)/shard_map/ppermute | solution.py:67
  119.8 6.0 %collective-permute-start.43 = (bf16[80,512]{1,0:T(8,128)(2,1)}, bf16[80,512]{1,0:T(8,128)(2,1)}, u32[]{:S(2)}, u32[]{:S(2)}) collective-permute-start(bf16[80,512]{1,0:T(8,128)(2,1)} %get-tuple-element.99), channel_id=1, source_target_pairs={{0,16},{4,20},{8,24},{12,28},{16,0},{20,4},{24,8},{28,12},{1,17},{... | collective-permute-start | bytes 245768 | tf_op jit(solution)/shard_map/ppermute | solution.py:67
  125.7 7.4 %collective-permute-done.18 = bf16[2,128,512]{2,1,0:T(8,128)(2,1)S(1)} collective-permute-done((bf16[2,128,512]{2,1,0:T(8,128)(2,1)S(1)}, bf16[2,128,512]{2,1,0:T(8,128)(2,1)S(1)}, u32[]{:S(2)}, u32[]{:S(2)}) %collective-permute-start.18) | collective-permute-done | bytes 262176 | tf_op jit(solution)/shard_map/ppermute | solution.py:67
  160.6 14.5 %collective-permute-done.21 = bf16[2,128,512]{2,1,0:T(8,128)(2,1)} collective-permute-done((bf16[2,128,512]{2,1,0:T(8,128)(2,1)}, bf16[2,128,512]{2,1,0:T(8,128)(2,1)}, u32[]{:S(2)}, u32[]{:S(2)}) %collective-permute-start.21) | collective-permute-done | bytes 262176 | tf_op jit(solution)/shard_map/ppermute | solution.py:67
  252.7 10.1 %collective-permute-done.30 = bf16[2,80,2048]{2,1,0:T(8,128)(2,1)} collective-permute-done((bf16[2,80,2048]{2,1,0:T(8,128)(2,1)}, bf16[2,80,2048]{2,1,0:T(8,128)(2,1)}, u32[]{:S(2)}, u32[]{:S(2)}) %collective-permute-start.30) | collective-permute-done | bytes 655392 | tf_op jit(solution)/shard_map/ppermute | solution.py:73
  279.0 7.2 %fusion.14 = f32[2,640,704]{1,2,0:T(8,128)S(1)} fusion(bf16[640,2048,1]{1,0,2:T(8,128)(2,1)S(1)} %bitcast.997, bf16[1,2048,2,704]{1,3,2,0:T(8,128)(2,1)} %param.23), kind=kOutput, calls=%fused_computation.40 | convolution fusion | flops 3690987520 | bytes 11993088 | tf_op jit(solution)/shard_map/rd,dkf->krf/dot_general | solution.py:342
  293.0 4.3 fusion.6
  298.8 7.6 %convolution_bitcast_fusion = f32[1,2048,2,704]{1,3,2,0:T(8,128)} fusion(bf16[640,2048,1]{1,0,2:T(8,128)(2,1)S(1)} %bitcast.998, bf16[640,1,704]{0,2,1:T(8,128)(2,1)S(1)} %get-tuple-element.36, bf16[640,1,704]{0,2,1:T(8,128)(2,1)S(1)} %get-tuple-element.22), kind=kOutput, calls=%fused_computation.12 | convolution fusion | flops 3694592000 | bytes 15958016 | tf_op jit(solution)/shard_map/rd,rkf->dkf/dot_general | solution.py:499
  309.6 15.1 %collective-permute-done.33 = bf16[2,80,2048]{2,1,0:T(8,128)(2,1)S(1)} collective-permute-done((bf16[2,80,2048]{2,1,0:T(8,128)(2,1)S(1)}, bf16[2,80,2048]{2,1,0:T(8,128)(2,1)S(1)}, u32[]{:S(2)}, u32[]{:S(2)}) %collective-permute-start.33) | collective-permute-done | bytes 655392 | tf_op jit(solution)/shard_map/ppermute | solution.py:73
  327.0 11.7 %collective-permute-done.49 = bf16[2,80,2176]{2,1,0:T(8,128)(2,1)S(1)} collective-permute-done((bf16[2,80,2176]{2,1,0:T(8,128)(2,1)S(1)}, bf16[2,80,2176]{2,1,0:T(8,128)(2,1)S(1)}, u32[]{:S(2)}, u32[]{:S(2)}) %collective-permute-start.49) | collective-permute-done | bytes 696352 | tf_op jit(solution)/shard_map/ppermute | solution.py:73
  343.1 7.4 %collective-permute-done.50 = bf16[80,2176]{1,0:T(8,128)(2,1)S(1)} collective-permute-done((bf16[80,2176]{1,0:T(8,128)(2,1)}, bf16[80,2176]{1,0:T(8,128)(2,1)S(1)}, u32[]{:S(2)}, u32[]{:S(2)}) %collective-permute-start.50) | collective-permute-done | bytes 348192 | tf_op jit(solution)/shard_map/ppermute | solution.py:70
  358.4 4.6 collective-permute-start.35
  375.6 5.0 convolution_bitcast_fusion.1
  395.3 3.9 collective-permute-start.58
  406.6 15.2 %collective-permute-done.57 = bf16[2,128,512]{2,1,0:T(8,128)(2,1)S(1)} collective-permute-done((bf16[2,128,512]{2,1,0:T(8,128)(2,1)S(1)}, bf16[2,128,512]{2,1,0:T(8,128)(2,1)S(1)}, u32[]{:S(2)}, u32[]{:S(2)}) %collective-permute-start.57) | collective-permute-done | bytes 262176 | tf_op jit(solution)/shard_map/ppermute | solution.py:67
  440.2 7.1 %collective-permute-start.65 = (bf16[272,512]{0,1:T(8,128)(2,1)S(1)}, bf16[272,512]{0,1:T(8,128)(2,1)S(1)}, u32[]{:S(2)}, u32[]{:S(2)}) collective-permute-start(bf16[272,512]{0,1:T(8,128)(2,1)S(1)} %get-tuple-element.96), channel_id=1, source_target_pairs={{0,16},{4,20},{8,24},{12,28},{16,0},{20,4},{24,8},{28,12},{1,17},{... | collective-permute-start | bytes 835592 | tf_op jit(solution)/shard_map/ppermute | solution.py:67
  447.2 22.2 %collective-permute-done.60 = bf16[2,128,512]{2,1,0:T(8,128)(2,1)} collective-permute-done((bf16[2,128,512]{2,1,0:T(8,128)(2,1)}, bf16[2,128,512]{2,1,0:T(8,128)(2,1)}, u32[]{:S(2)}, u32[]{:S(2)}) %collective-permute-start.60) | collective-permute-done | bytes 262176 | tf_op jit(solution)/shard_map/ppermute | solution.py:67
  479.6 5.3 collective-permute-done.65
  515.9 4.7 collective-permute-done.67
  542.7 13.5 %collective-permute-done.74 = bf16[4,256,512]{2,1,0:T(8,128)(2,1)S(1)} collective-permute-done((bf16[4,256,512]{2,1,0:T(8,128)(2,1)S(1)}, bf16[4,256,512]{2,1,0:T(8,128)(2,1)S(1)}, u32[]{:S(2)}, u32[]{:S(2)}) %collective-permute-start.74) | collective-permute-done | bytes 1048608 | tf_op jit(solution)/shard_map/ppermute | solution.py:70
  (880 shorter events, 341.9 us)
Async XLA Ops:
  11.9 40.7 %collective-permute-start = (bf16[128,512]{1,0:T(8,128)(2,1)}, bf16[128,512]{1,0:T(8,128)(2,1)S(1)}, u32[]{:S(2)}, u32[]{:S(2)}) collective-permute-start(bf16[128,512]{1,0:T(8,128)(2,1)} %param.14), channel_id=1, source_target_pairs={{0,0},{1,8},{2,16},{3,24},{4,4},{5,12},{6,20},{7,28},{8,1},{9,9},{... | collective-permute-start | bytes 393224 | tf_op jit(solution)/shard_map/ppermute | solution.py:81
  18.9 66.7 %collective-permute-start.16 = (bf16[4,256,512]{2,1,0:T(8,128)(2,1)}, bf16[4,256,512]{2,1,0:T(8,128)(2,1)}, u32[]{:S(2)}, u32[]{:S(2)}) collective-permute-start(bf16[4,256,512]{2,1,0:T(8,128)(2,1)} %param.19), channel_id=1, source_target_pairs={{0,4},{4,0},{8,12},{12,8},{16,20},{20,16},{24,28},{28,24},{1,5},{5... | collective-permute-start | bytes 3145736 | tf_op jit(solution)/shard_map/ppermute | solution.py:70
  23.0 54.9 %collective-permute-start.10 = (bf16[2,256,512]{2,1,0:T(8,128)(2,1)}, bf16[2,256,512]{2,1,0:T(8,128)(2,1)}, u32[]{:S(2)}, u32[]{:S(2)}) collective-permute-start(bf16[2,256,512]{2,1,0:T(8,128)(2,1)} %param.18), channel_id=1, source_target_pairs={{0,4},{4,0},{8,12},{12,8},{16,20},{20,16},{24,28},{28,24},{1,5},{5... | collective-permute-start | bytes 1572872 | tf_op jit(solution)/shard_map/ppermute | solution.py:70
  30.5 60.9 %collective-permute-start.39 = (bf16[128,512]{1,0:T(8,128)(2,1)}, bf16[128,512]{1,0:T(8,128)(2,1)}, u32[]{:S(2)}, u32[]{:S(2)}) collective-permute-start(bf16[128,512]{1,0:T(8,128)(2,1)} %param.15), channel_id=1, source_target_pairs={{0,0},{1,8},{2,16},{3,24},{4,4},{5,12},{6,20},{7,28},{8,1},{9,9},{... | collective-permute-start | bytes 393224 | tf_op jit(solution)/shard_map/ppermute | solution.py:81
  82.5 35.8 %collective-permute-start.12 = (bf16[2,128,512]{2,1,0:T(8,128)(2,1)S(1)}, bf16[2,128,512]{2,1,0:T(8,128)(2,1)S(1)}, u32[]{:S(2)}, u32[]{:S(2)}) collective-permute-start(bf16[2,128,512]{2,1,0:T(8,128)(2,1)S(1)} %get-tuple-element.78), channel_id=1, source_target_pairs={{0,16},{4,20},{8,24},{12,28},{16,0},{20,4},{24,8},{28,12},{1,17},{... | collective-permute-start | bytes 786440 | tf_op jit(solution)/shard_map/ppermute | solution.py:67
  83.1 35.8 %collective-permute-start.11 = (bf16[2,128,512]{2,1,0:T(8,128)(2,1)S(1)}, bf16[2,128,512]{2,1,0:T(8,128)(2,1)S(1)}, u32[]{:S(2)}, u32[]{:S(2)}) collective-permute-start(bf16[2,128,512]{2,1,0:T(8,128)(2,1)S(1)} %get-tuple-element.76), channel_id=1, source_target_pairs={{0,8},{4,12},{8,0},{12,4},{16,24},{20,28},{24,16},{28,20},{1,9},{5... | collective-permute-start | bytes 786440 | tf_op jit(solution)/shard_map/ppermute | solution.py:67
  89.3 30.4 %collective-permute-start.19 = (bf16[2,128,512]{2,1,0:T(8,128)(2,1)S(1)}, bf16[2,128,512]{2,1,0:T(8,128)(2,1)S(1)}, u32[]{:S(2)}, u32[]{:S(2)}) collective-permute-start(bf16[2,128,512]{2,1,0:T(8,128)(2,1)S(1)} %get-tuple-element.74), channel_id=1, source_target_pairs={{0,24},{4,28},{8,16},{12,20},{16,8},{20,12},{24,0},{28,4},{1,25},{... | collective-permute-start | bytes 786440 | tf_op jit(solution)/shard_map/ppermute | solution.py:67
  91.4 41.6 %collective-permute-start.18 = (bf16[2,128,512]{2,1,0:T(8,128)(2,1)S(1)}, bf16[2,128,512]{2,1,0:T(8,128)(2,1)S(1)}, u32[]{:S(2)}, u32[]{:S(2)}) collective-permute-start(bf16[2,128,512]{2,1,0:T(8,128)(2,1)S(1)} %get-tuple-element.75), channel_id=1, source_target_pairs={{0,16},{4,20},{8,24},{12,28},{16,0},{20,4},{24,8},{28,12},{1,17},{... | collective-permute-start | bytes 786440 | tf_op jit(solution)/shard_map/ppermute | solution.py:67
  91.6 41.4 %collective-permute-start.17 = (bf16[2,128,512]{2,1,0:T(8,128)(2,1)S(1)}, bf16[2,128,512]{2,1,0:T(8,128)(2,1)S(1)}, u32[]{:S(2)}, u32[]{:S(2)}) collective-permute-start(bf16[2,128,512]{2,1,0:T(8,128)(2,1)S(1)} %get-tuple-element.73), channel_id=1, source_target_pairs={{0,8},{4,12},{8,0},{12,4},{16,24},{20,28},{24,16},{28,20},{1,9},{5... | collective-permute-start | bytes 786440 | tf_op jit(solution)/shard_map/ppermute | solution.py:67
  118.3 64.6 %collective-permute-start.23 = (bf16[4,256,512]{2,1,0:T(8,128)(2,1)}, bf16[4,256,512]{2,1,0:T(8,128)(2,1)}, u32[]{:S(2)}, u32[]{:S(2)}) collective-permute-start(bf16[4,256,512]{2,1,0:T(8,128)(2,1)} %param.20), channel_id=1, source_target_pairs={{0,4},{4,0},{8,12},{12,8},{16,20},{20,16},{24,28},{28,24},{1,5},{5... | collective-permute-start | bytes 3145736 | tf_op jit(solution)/shard_map/ppermute | solution.py:70
  118.8 31.2 %collective-permute-start.44 = (bf16[80,512]{1,0:T(8,128)(2,1)}, bf16[80,512]{1,0:T(8,128)(2,1)}, u32[]{:S(2)}, u32[]{:S(2)}) collective-permute-start(bf16[80,512]{1,0:T(8,128)(2,1)} %get-tuple-element.98), channel_id=1, source_target_pairs={{0,24},{4,28},{8,16},{12,20},{16,8},{20,12},{24,0},{28,4},{1,25},{... | collective-permute-start | bytes 245768 | tf_op jit(solution)/shard_map/ppermute | solution.py:67
  119.8 32.8 %collective-permute-start.43 = (bf16[80,512]{1,0:T(8,128)(2,1)}, bf16[80,512]{1,0:T(8,128)(2,1)}, u32[]{:S(2)}, u32[]{:S(2)}) collective-permute-start(bf16[80,512]{1,0:T(8,128)(2,1)} %get-tuple-element.99), channel_id=1, source_target_pairs={{0,16},{4,20},{8,24},{12,28},{16,0},{20,4},{24,8},{28,12},{1,17},{... | collective-permute-start | bytes 245768 | tf_op jit(solution)/shard_map/ppermute | solution.py:67
  150.0 25.0 %collective-permute-start.21 = (bf16[2,128,512]{2,1,0:T(8,128)(2,1)}, bf16[2,128,512]{2,1,0:T(8,128)(2,1)}, u32[]{:S(2)}, u32[]{:S(2)}) collective-permute-start(bf16[2,128,512]{2,1,0:T(8,128)(2,1)} %multiply_convert_fusion.9), channel_id=1, source_target_pairs={{0,16},{4,20},{8,24},{12,28},{16,0},{20,4},{24,8},{28,12},{1,17},{... | collective-permute-start | bytes 786440 | tf_op jit(solution)/shard_map/ppermute | solution.py:67
  152.5 22.6 %collective-permute-start.20 = (bf16[2,128,512]{2,1,0:T(8,128)(2,1)}, bf16[2,128,512]{2,1,0:T(8,128)(2,1)}, u32[]{:S(2)}, u32[]{:S(2)}) collective-permute-start(bf16[2,128,512]{2,1,0:T(8,128)(2,1)} %multiply_convert_fusion.9), channel_id=1, source_target_pairs={{0,8},{4,12},{8,0},{12,4},{16,24},{20,28},{24,16},{28,20},{1,9},{5... | collective-permute-start | bytes 786440 | tf_op jit(solution)/shard_map/ppermute | solution.py:67
  239.8 24.6 %collective-permute-start.47 = (bf16[2,2,80,2048]{3,2,1,0:T(8,128)(2,1)}, bf16[2,2,80,2048]{3,2,1,0:T(8,128)(2,1)}, u32[]{:S(2)}, u32[]{:S(2)}) collective-permute-start(bf16[2,2,80,2048]{3,2,1,0:T(8,128)(2,1)} %pad_maximum_fusion.9), channel_id=1, source_target_pairs={{0,1},{1,0},{2,3},{3,2},{4,5},{5,4},{6,7},{7,6},{8,9},{9,8},{10,11... | collective-permute-start | bytes 3932168 | tf_op jit(solution)/shard_map/ppermute | solution.py:73
  309.1 29.7 %collective-permute-start.49 = (bf16[2,80,2176]{2,1,0:T(8,128)(2,1)S(1)}, bf16[2,80,2176]{2,1,0:T(8,128)(2,1)S(1)}, u32[]{:S(2)}, u32[]{:S(2)}) collective-permute-start(bf16[2,80,2176]{2,1,0:T(8,128)(2,1)S(1)} %fusion.65), channel_id=1, source_target_pairs={{0,2},{1,3},{2,0},{3,1},{4,6},{5,7},{6,4},{7,5},{8,10},{9,11},{10,... | collective-permute-start | bytes 2088968 | tf_op jit(solution)/shard_map/ppermute | solution.py:73
  399.3 22.5 %collective-permute-start.57 = (bf16[2,128,512]{2,1,0:T(8,128)(2,1)S(1)}, bf16[2,128,512]{2,1,0:T(8,128)(2,1)S(1)}, u32[]{:S(2)}, u32[]{:S(2)}) collective-permute-start(bf16[2,128,512]{2,1,0:T(8,128)(2,1)S(1)} %get-tuple-element.68), channel_id=1, source_target_pairs={{0,16},{4,20},{8,24},{12,28},{16,0},{20,4},{24,8},{28,12},{1,17},{... | collective-permute-start | bytes 786440 | tf_op jit(solution)/shard_map/ppermute | solution.py:67
  401.0 134.4 %collective-permute-start.75 = (bf16[4,256,512]{2,1,0:T(8,128)(2,1)}, bf16[4,256,512]{2,1,0:T(8,128)(2,1)}, u32[]{:S(2)}, u32[]{:S(2)}) collective-permute-start(bf16[4,256,512]{2,1,0:T(8,128)(2,1)} %pad_maximum_fusion.15), channel_id=1, source_target_pairs={{0,4},{4,0},{8,12},{12,8},{16,20},{20,16},{24,28},{28,24},{1,5},{5... | collective-permute-start | bytes 3145736 | tf_op jit(solution)/shard_map/ppermute | solution.py:70
  429.6 39.8 %collective-permute-start.60 = (bf16[2,128,512]{2,1,0:T(8,128)(2,1)}, bf16[2,128,512]{2,1,0:T(8,128)(2,1)}, u32[]{:S(2)}, u32[]{:S(2)}) collective-permute-start(bf16[2,128,512]{2,1,0:T(8,128)(2,1)} %get-tuple-element.85), channel_id=1, source_target_pairs={{0,16},{4,20},{8,24},{12,28},{16,0},{20,4},{24,8},{28,12},{1,17},{... | collective-permute-start | bytes 786440 | tf_op jit(solution)/shard_map/ppermute | solution.py:67
  429.6 39.8 %collective-permute-start.59 = (bf16[2,128,512]{2,1,0:T(8,128)(2,1)}, bf16[2,128,512]{2,1,0:T(8,128)(2,1)}, u32[]{:S(2)}, u32[]{:S(2)}) collective-permute-start(bf16[2,128,512]{2,1,0:T(8,128)(2,1)} %get-tuple-element.85), channel_id=1, source_target_pairs={{0,8},{4,12},{8,0},{12,4},{16,24},{20,28},{24,16},{28,20},{1,9},{5... | collective-permute-start | bytes 786440 | tf_op jit(solution)/shard_map/ppermute | solution.py:67
  437.4 42.1 %collective-permute-start.66 = (bf16[272,512]{0,1:T(8,128)(2,1)S(1)}, bf16[272,512]{0,1:T(8,128)(2,1)S(1)}, u32[]{:S(2)}, u32[]{:S(2)}) collective-permute-start(bf16[272,512]{0,1:T(8,128)(2,1)S(1)} %get-tuple-element.96), channel_id=1, source_target_pairs={{0,24},{4,28},{8,16},{12,20},{16,8},{20,12},{24,0},{28,4},{1,25},{... | collective-permute-start | bytes 835592 | tf_op jit(solution)/shard_map/ppermute | solution.py:67
  440.2 44.8 %collective-permute-start.65 = (bf16[272,512]{0,1:T(8,128)(2,1)S(1)}, bf16[272,512]{0,1:T(8,128)(2,1)S(1)}, u32[]{:S(2)}, u32[]{:S(2)}) collective-permute-start(bf16[272,512]{0,1:T(8,128)(2,1)S(1)} %get-tuple-element.96), channel_id=1, source_target_pairs={{0,16},{4,20},{8,24},{12,28},{16,0},{20,4},{24,8},{28,12},{1,17},{... | collective-permute-start | bytes 835592 | tf_op jit(solution)/shard_map/ppermute | solution.py:67
  474.9 63.6 %collective-permute-start.73 = (bf16[2,256,512]{2,1,0:T(8,128)(2,1)}, bf16[2,256,512]{2,1,0:T(8,128)(2,1)}, u32[]{:S(2)}, u32[]{:S(2)}) collective-permute-start(bf16[2,256,512]{2,1,0:T(8,128)(2,1)} %pad_maximum_fusion.21), channel_id=1, source_target_pairs={{0,4},{4,0},{8,12},{12,8},{16,20},{20,16},{24,28},{28,24},{1,5},{5... | collective-permute-start | bytes 1572872 | tf_op jit(solution)/shard_map/ppermute | solution.py:70
  531.2 25.0 %collective-permute-start.74 = (bf16[4,256,512]{2,1,0:T(8,128)(2,1)S(1)}, bf16[4,256,512]{2,1,0:T(8,128)(2,1)S(1)}, u32[]{:S(2)}, u32[]{:S(2)}) collective-permute-start(bf16[4,256,512]{2,1,0:T(8,128)(2,1)S(1)} %pad_maximum_fusion.14), channel_id=1, source_target_pairs={{0,4},{4,0},{8,12},{12,8},{16,20},{20,16},{24,28},{28,24},{1,5},{5... | collective-permute-start | bytes 3145736 | tf_op jit(solution)/shard_map/ppermute | solution.py:70
  (230 other events, 2139.4 us)

commit v2 on v1

--- a/solution.py
+++ b/solution.py
@@ -1,6 +1,8 @@
 import jax
 import jax.numpy as jnp
 from jax import lax
+from jax.experimental import pallas as pl
+from jax.experimental.pallas import tpu as pltpu
 from jax.sharding import PartitionSpec as P
 
 HS = 128
@@ -30,6 +32,257 @@
         values = jnp.where((amount & bit) != 0, flipped, values)
         bit *= 2
     return values
+
+
+NN = (((1,), (0,)), ((), ()))
+NT = (((1,), (1,)), ((), ()))
+TN = (((0,), (0,)), ((), ()))
+
+
+def mul(left, right, form):
+    return lax.dot_general(left, right, form, preferred_element_type=F32)
+
+
+def shape(dims, dtype):
+    return jax.ShapeDtypeStruct(tuple(dims), dtype)
+
+
+def run(name, body, outs, args, scratch=()):
+    vector = pl.BlockSpec(memory_space=pltpu.VMEM)
+    return pl.pallas_call(
+        body,
+        out_shape=tuple(outs),
+        in_specs=[pl.BlockSpec(memory_space=pltpu.SMEM)] + [vector] * (len(args) - 1),
+        out_specs=tuple(vector for _ in outs),
+        scratch_shapes=list(scratch),
+        name=name,
+    )(*args)
+
+
+def place(store, parts, sub, first=0):
+    for j, part in enumerate(parts):
+        rows = part.shape[1]
+        start = pl.multiple_of((sub ^ j) * rows, rows)
+        for a in range(part.shape[0]):
+            store[first + a, pl.ds(start, rows), :] = part[a]
+
+
+def block(index):
+    return pl.ds(pl.multiple_of(index * TOK, TOK), TOK)
+
+
+def send_blocks(total, outs, order):
+    for k in range(E):
+        for a in range(total.shape[0]):
+            outs[k][a] = total[a, block(order ^ k), :].astype(outs[k].dtype)
+
+
+def key_value_body(subs):
+    def body(at, *refs):
+        rows, gain, parts = refs[:E], refs[E], refs[E + 1 : E + 1 + subs]
+        gained, *outs = refs[E + 1 + subs : E + 2 + subs + E]
+        weights, total = refs[E + 2 + subs + E :]
+        place(weights, parts, at[1])
+        for q in range(E):
+            gained[q * TOK : (q + 1) * TOK, :] = (rows[q][...].astype(F32) * gain[...]).astype(BF16)
+        for a in range(2):
+            total[a] = mul(gained[...], weights[a], NN)
+        send_blocks(total, outs, at[0])
+
+    return body
+
+
+def routed_body(subs, joined):
+    count = 1 if joined else E
+
+    def body(at, *refs):
+        rows, hot, parts = refs[:count], refs[count], refs[count + 1 : count + 1 + subs]
+        rest = refs[count + 1 + subs :]
+        if joined:
+            wide = rows[0]
+        else:
+            wide, rest = rest[0], rest[1:]
+            for q in range(E):
+                wide[q * TOK : (q + 1) * TOK, :] = rows[q][...]
+        outs, weights, total = rest[:E], rest[E], rest[E + 1]
+        place(weights, parts, at[1])
+        for e in range(E):
+            every = mul(wide[...], weights[e], NN)
+            for i in range(TOPK):
+                mine = every * hot[:, i * E + e : i * E + e + 1]
+                total[i] = mine if e == 0 else total[i] + mine
+        send_blocks(total, outs, at[0])
+
+    return body
+
+
+def spread_pairs(at, rows, hot, out):
+    for k in range(E):
+        where = block(at[0] ^ k)
+        mask = hot[where, :].astype(BF16)
+        for e in range(E):
+            out[e, where, :] = (
+                rows[k][0] * mask[:, e : e + 1] + rows[k][1] * mask[:, E + e : E + e + 1]
+            )
+
+
+def fold_out(total, keep_0, keep_2, send):
+    keep_0[...] = total[0:TOK]
+    keep_2[...] = total[2 * TOK : 3 * TOK]
+    send[0] = total[TOK : 2 * TOK].astype(BF16)
+    send[1] = total[3 * TOK : 4 * TOK].astype(BF16)
+
+
+def output_body(subs):
+    def body(at, *refs):
+        rows, hot, parts = refs[:E], refs[E], refs[E + 1 : E + 1 + subs]
+        mixed, keep_0, keep_2, send, weights = refs[E + 1 + subs :]
+        place(weights, parts, at[1])
+        spread_pairs(at, rows, hot, mixed)
+        total = mul(mixed[0], weights[0], NT)
+        for e in range(1, E):
+            total = total + mul(mixed[e], weights[e], NT)
+        fold_out(total, keep_0, keep_2, send)
+
+    return body
+
+
+def spread_body(at, *refs):
+    spread_pairs(at, refs[:E], refs[E], refs[E + 1])
+
+
+def input_body(subs):
+    def body(at, *refs):
+        rows, dmixed = refs[:E], refs[E]
+        kv_parts = refs[E + 1 : E + 1 + subs]
+        query_parts = refs[E + 1 + subs : E + 1 + 2 * subs]
+        dkv_all, keep_0, keep_2, send, weights = refs[E + 1 + 2 * subs :]
+        place(weights, kv_parts, at[1])
+        place(weights, query_parts, at[1], 2)
+        for k in range(E):
+            for a in range(2):
+                dkv_all[a, block(at[0] ^ k), :] = rows[k][a]
+        total = mul(dkv_all[0], weights[0], NT) + mul(dkv_all[1], weights[1], NT)
+        for e in range(E):
+            total = total + mul(dmixed[e], weights[2 + e], NT)
+        fold_out(total, keep_0, keep_2, send)
+
+    return body
+
+
+def weight_grad_body(at, rows, other, *refs):
+    parts, total = refs[:-1], refs[-1]
+    for a in range(other.shape[0]):
+        total[...] = mul(rows[...], other[a], TN)
+        for j, part in enumerate(parts):
+            count = part.shape[1]
+            start = pl.multiple_of((at[1] ^ j) * count, count)
+            part[a] = total[pl.ds(start, count), :].astype(part.dtype)
+
+
+def attention_mask(at):
+    row = lax.broadcasted_iota(jnp.int32, (TOK, TOK), 0)
+    col = lax.broadcasted_iota(jnp.int32, (TOK, TOK), 1)
+    row_doc, col_doc, end = jnp.zeros_like(row), jnp.zeros_like(row), 0
+    for d in range(4):
+        end = end + at[d]
+        row_doc = row_doc + (row >= end).astype(jnp.int32)
+        col_doc = col_doc + (col >= end).astype(jnp.int32)
+    return (row_doc == col_doc) & (col <= row)
+
+
+def attention_body(at, own_kv, *refs):
+    got_kv, own_query, got_query = refs[: E - 1], refs[E - 1], refs[E : 2 * E - 1]
+    cols, low, probs, context, gated = refs[2 * E - 1 :]
+    scale = cols[:, 0:1]
+    for a in range(4):
+        own, got = (own_kv, got_kv) if a < 2 else (own_query, got_query)
+        total = own[a % 2]
+        for one in got:
+            total = total + one[a % 2].astype(F32)
+        low[a] = (total * scale).astype(BF16)
+    allowed = attention_mask(at)
+    for h in range(low.shape[2] // HS):
+        head = slice(h * HS, (h + 1) * HS)
+        for i in range(TOPK):
+            scores = mul(low[2 + i, :, head], low[0, :, head], NT) * HS ** (-0.5)
+            scores = jnp.where(allowed, scores, NEGATIVE)
+            top = jnp.exp(scores - jnp.max(scores, axis=-1, keepdims=True))
+            prob = top / jnp.sum(top, axis=-1, keepdims=True)
+            probs[h, i * TOK : (i + 1) * TOK, :] = prob
+            mixed = mul(prob.astype(BF16), low[1, :, head], NN).astype(BF16)
+            context[i, :, head] = mixed
+            gated[i, :, head] = (mixed.astype(F32) * cols[:, 1 + i : 2 + i]).astype(BF16)
+
+
+def attention_back_body(at, own, *refs):
+    got = refs[: E - 1]
+    cols, low, probs, context, dquery, dkey_val, sums = refs[E - 1 :]
+    scale = cols[:, 0:1]
+    inner = jnp.zeros((TOK, 1), F32)
+    dprob = []
+    dcontext = []
+    for i in range(TOPK):
+        raw = own[i]
+        for one in got:
+            raw = raw + one[i].astype(F32)
+        dprob.append(jnp.sum(context[i].astype(F32) * raw, axis=-1, keepdims=True))
+        dcontext.append((raw * cols[:, 1 + i : 2 + i]).astype(BF16))
+    for h in range(low.shape[2] // HS):
+        head = slice(h * HS, (h + 1) * HS)
+        key, value = low[0, :, head], low[1, :, head]
+        dkey = jnp.zeros((TOK, HS), F32)
+        dvalue = jnp.zeros((TOK, HS), F32)
+        for i in range(TOPK):
+            query = low[2 + i, :, head]
+            grad = dcontext[i][:, head]
+            prob = probs[h, i * TOK : (i + 1) * TOK, :]
+            dweight = mul(grad, value, NT)
+            dscore = prob * (dweight - jnp.sum(prob * dweight, axis=-1, keepdims=True))
+            dscore = dscore.astype(BF16)
+            done = mul(dscore, key, NN) * HS ** (-0.5)
+            dkey = dkey + mul(dscore, query, TN)
+            dvalue = dvalue + mul(prob.astype(BF16), grad, TN)
+            inner = inner + jnp.sum(done * query.astype(F32), axis=-1, keepdims=True)
+            dquery[i, :, head] = (done * scale).astype(BF16)
+        dkey = dkey * HS ** (-0.5)
+        inner = inner + jnp.sum(
+            dkey * key.astype(F32) + dvalue * value.astype(F32), axis=-1, keepdims=True
+        )
+        dkey_val[0, :, head] = (dkey * scale).astype(BF16)
+        dkey_val[1, :, head] = (dvalue * scale).astype(BF16)
+    lane = lax.broadcasted_iota(jnp.int32, (TOK, TOK), 1)
+    table = jnp.where(lane == 0, dprob[0], jnp.where(lane == 1, dprob[1], jnp.where(lane == 2, inner, 0.0)))
+    sums[...] = jnp.transpose(table)[0:8]
+
+
+def join_body(at, *refs):
+    pieces, out = refs[:E], refs[E]
+    size = pieces[0].shape[1]
+    for k in range(E):
+        for p in range(E):
+
+            @pl.when((at[2] ^ k) == p)
+            def _(k=k, p=p):
+                out[:, p * size : (p + 1) * size] = pieces[k][...]
+
+
+def split_body(extra):
+    def body(at, own, got, *refs):
+        outs, store = refs[:E], refs[E]
+        store[...] = (own[...] + got[...].astype(F32)).astype(BF16)
+        size = outs[0].shape[1] - extra
+        for k in range(E):
+            for p in range(E):
+
+                @pl.when((at[2] ^ k) == p)
+                def _(k=k, p=p):
+                    outs[k][:, :size] = store[:, p * size : (p + 1) * size]
+
+            if extra:
+                outs[k][:, size:] = store[:, E * size :]
+
+    return body
 
 
 def local(
@@ -94,21 +347,25 @@
         return parts
 
     def reduce_subs(parts):
-        bit = subs // 2
+        bit = len(parts) // 2
         while bit >= 1:
             parts = [parts[j] + by_sub(parts[j + bit].astype(BF16), bit).astype(F32) for j in range(bit)]
             bit //= 2
         return parts[0]
 
     def gather_narrow(values):
-        two = jnp.stack([values, by_narrow(values, 2)])
-        one = by_narrow(two, 1)
-        return jnp.stack([two[0], one[0], two[1], one[1]])
-
-    def reduce_narrow(parts):
-        low = parts.astype(BF16)
-        two = jnp.stack([parts[0], parts[1]]) + by_narrow(low[2:4], 2).astype(F32)
-        return two[0] + by_narrow(two[1].astype(BF16), 1).astype(F32)
+        other = by_narrow(values, 2)
+        return [values, by_narrow(values, 1), other, by_narrow(other, 1)]
+
+    def reduce_narrow(keep_0, keep_2, send):
+        got = by_narrow(send, 1)
+        other = by_narrow((keep_2 + got[1].astype(F32)).astype(BF16), 2)
+        return keep_0 + got[0].astype(F32) + other.astype(F32)
+
+    def finish_subs(keep, send):
+        bit = len(keep)
+        keep = [keep[j] + by_sub(send[j], bit).astype(F32) for j in range(bit)]
+        return reduce_subs(keep)
 
     def sum_narrow(values):
         values = values + by_narrow(values, 2)
@@ -134,9 +391,13 @@
     used = packed.shape[0]
     packed = jnp.pad(packed, ((0, -used % 16), (0, 0)))
     parts = gather_subs(packed)
-    by_k = [gather_planes(one) for one in parts]
-    table = jnp.stack([by_k[j][k] for k in range(E) for j in range(subs)])
+    table = jnp.stack(gather_planes(jnp.stack(parts)))
+    table = table.reshape((wide_count,) + packed.shape)
     table = xor_shuffle(table, wide)
+    near = xor_shuffle(jnp.stack(parts), sub)
+    gain_one_plane = near[:, 0].reshape(slice_width).astype(F32)
+    gain_two_plane = near[:, 5].reshape(slice_width).astype(F32)
+    router_two_plane = near[:, 6:10].swapaxes(0, 1).reshape(E, slice_width).astype(F32)
     gain_one = table[:, 0].reshape(width).astype(F32)
     router_one = table[:, 1:5].swapaxes(0, 1).reshape(E, width)
     gain_two = table[:, 5].reshape(width).astype(F32)
@@ -184,7 +445,10 @@
 
     hot_k = hot[:, 0].reshape(E, subs, 2, TOK, E)
     hot_k = lax.dynamic_index_in_dim(hot_k, sub, 1, False)
-    hot_k = xor_shuffle(hot_k, plane)
+    hot_q = xor_shuffle(hot_k, narrow)
+    hot_cols = hot_q.transpose(0, 2, 1, 3).reshape(E * TOK, TOPK * E)
+    hot_two_k = xor_shuffle(jnp.moveaxis(hot_two, -1, 0), plane)
+    at = jnp.stack([narrow ^ plane, sub, plane, narrow]).astype(jnp.int32)
 
     kv_parts = gather_subs(key_value)
     query_parts = gather_subs(query_proj)
@@ -192,54 +456,38 @@
     turned_stream = swap(stream)
     turned_grad = swap(out_grad)
 
-    def widen(values):
-        everyone = xor_shuffle(gather_narrow(values), narrow ^ plane)
-        pieces = everyone.reshape(E, TOK, subs, shard_rows).transpose(2, 0, 1, 3)
-        return xor_shuffle(pieces, sub)
-
     def own_slice(vector, place):
         return lax.dynamic_slice_in_dim(vector, place * slice_width, slice_width, vector.ndim - 1)
 
-    gain_one_plane = own_slice(gain_one, plane)
-    gain_two_plane = own_slice(gain_two, plane)
-    router_two_plane = own_slice(router_two, plane).astype(F32)
     gain_one_home = own_slice(gain_one, narrow)
     router_one_home = own_slice(router_one, narrow).astype(F32)
 
-    wide_stream = widen(turned_stream)
-    gain_pieces = xor_shuffle(gain_one_plane.reshape(subs, shard_rows), sub)
-    gained = (wide_stream.astype(F32) * gain_pieces[:, None, None, :]).astype(BF16)
-    gained = gained.reshape(subs, E * TOK, shard_rows)
-
-    def project(rows, weights):
-        total = None
-        for j in range(subs):
-            one = jnp.einsum("td,adc->atc", rows[j], weights[j], preferred_element_type=F32)
-            total = one if total is None else total + one
-        return total
-
-    def choose(every):
-        shaped = every.reshape(E, E, TOK, -1)
-        pairs = []
-        for k2 in range(TOPK):
-            mask = hot_k[:, k2]
-            total = jnp.where(mask[:, :, 0:1] > 0, shaped[0], 0.0)
-            for e in range(1, E):
-                total = jnp.where(mask[:, :, e : e + 1] > 0, shaped[e], total)
-            pairs.append(total)
-        return jnp.stack(pairs, axis=1)
-
-    def scatter_planes(partial):
-        got = exchange_planes([None] + [partial[k].astype(BF16) for k in range(1, E)])
-        total = partial[0]
-        for k in range(1, E):
-            total = total + got[k].astype(F32)
-        return total
-
-    kv_partial = project(gained, kv_parts).reshape(2, E, TOK, local_width).swapaxes(0, 1)
-    key_val = scatter_planes(kv_partial)
-    query_partial = choose(project(gained, query_parts))
-    query_raw = scatter_planes(query_partial)
+    rows_all = E * TOK
+    sent = shape((2, TOK, local_width), BF16)
+    kept_own = shape((2, TOK, local_width), F32)
+    gained, *kv_blocks = run(
+        "key_value",
+        key_value_body(subs),
+        [shape((rows_all, slice_width), BF16), kept_own] + [sent] * (E - 1),
+        [at, *gather_narrow(turned_stream), gain_one_plane[None], *kv_parts],
+        [
+            pltpu.VMEM((2, slice_width, local_width), BF16),
+            pltpu.VMEM((2, rows_all, local_width), F32),
+        ],
+    )
+    kv_blocks = exchange_planes(kv_blocks)
+    routed_scratch = [
+        pltpu.VMEM((E, slice_width, local_width), BF16),
+        pltpu.VMEM((TOPK, rows_all, local_width), F32),
+    ]
+    query_blocks = run(
+        "query",
+        routed_body(subs, True),
+        [kept_own] + [sent] * (E - 1),
+        [at, gained, hot_cols, *query_parts],
+        routed_scratch,
+    )
+    query_blocks = exchange_planes(query_blocks)
 
     gained_home = home_stream * gain_one_home
     stats_one = jnp.concatenate(
@@ -260,61 +508,44 @@
 
     prob_one = gates(logits_one, hot_one)
     gate_one = prob_one * keep_one
-    key_val = (key_val * scale_one[None, :, None]).astype(BF16)
-    query = (query_raw * scale_one[None, :, None]).astype(BF16)
-
-    doc_ends = jnp.cumsum(doc_lengths[0])
-    positions = jnp.arange(TOK, dtype=jnp.int32)
-    member = jnp.sum((positions[:, None] >= doc_ends[None, :]).astype(jnp.int32), axis=1)
-    allowed = (member[:, None] == member[None, :]) & (positions[None, :] <= positions[:, None])
-    allowed = jnp.concatenate([allowed, allowed], axis=0)
-    query_rows = query.reshape(TOPK * TOK, head_count, HS)
-    key_rows = key_val[0].reshape(TOK, head_count, HS)
-    value_rows = key_val[1].reshape(TOK, head_count, HS)
-    scores = (
-        jnp.einsum("rhc,jhc->hrj", query_rows, key_rows, preferred_element_type=F32) * score_scale
-    )
-    scores = jnp.where(allowed[None], scores, NEGATIVE)
-    exp_scores = jnp.exp(scores - jnp.max(scores, axis=-1, keepdims=True))
-    probs = exp_scores / jnp.sum(exp_scores, axis=-1, keepdims=True)
-    probs_low = probs.astype(BF16)
-    context = jnp.einsum("hrj,jhc->rhc", probs_low, value_rows, preferred_element_type=F32).astype(BF16)
-    context = context.reshape(TOPK, TOK, local_width)
-    gated = (context.astype(F32) * gate_one[:, :, None]).astype(BF16)
+
+    token_cols = jnp.stack([scale_one, gate_one[0], gate_one[1]] + [scale_one] * 5, axis=1)
+    low, probs, context, gated = run(
+        "attention",
+        attention_body,
+        [
+            shape((4, TOK, local_width), BF16),
+            shape((head_count, TOPK * TOK, TOK), F32),
+            sent,
+            sent,
+        ],
+        [doc_lengths[0], *kv_blocks, *query_blocks, token_cols],
+    )
 
     out_parts = gather_subs(output_proj)
 
-    def spread(pairs):
-        result = []
-        for e in range(E):
-            first = jnp.where(hot_k[:, 0, :, e : e + 1] > 0, pairs[:, 0], jnp.zeros((), BF16))
-            one = jnp.where(hot_k[:, 1, :, e : e + 1] > 0, pairs[:, 1], first)
-            result.append(one.reshape(E * TOK, -1))
-        return result
-
-    def back(rows, weights):
-        total = None
-        for a in range(len(rows)):
-            one = dot(rows[a], weights[a], ((1,), (1,)))
-            total = one if total is None else total + one
-        return total
-
-    def to_turned(pieces):
-        by_block = jnp.stack(pieces).reshape(subs, E, TOK, shard_rows).transpose(1, 0, 2, 3)
-        by_block = xor_shuffle(by_block, narrow ^ plane)
-        total = xor_shuffle(reduce_narrow(by_block), sub)
-        return total.transpose(1, 0, 2).reshape(TOK, slice_width)
-
-    mixed = spread(jnp.stack(gather_planes(gated)))
-    attention = to_turned([back(mixed, out_parts[j]) for j in range(subs)])
-    hidden = turned_stream.astype(F32) + attention
+    folded = [shape((TOK, slice_width), F32), shape((TOK, slice_width), F32), shape((2, TOK, slice_width), BF16)]
+    mixed, *attention = run(
+        "output",
+        output_body(subs),
+        [shape((E, rows_all, local_width), BF16)] + folded,
+        [at, *gather_planes(gated), hot_cols, *out_parts],
+        [pltpu.VMEM((E, slice_width, local_width), BF16)],
+    )
+    hidden = turned_stream.astype(F32) + reduce_narrow(*attention)
 
     def dispatch(rows):
         picked = jnp.einsum("kst,td->ksd", select, rows, preferred_element_type=F32).astype(BF16)
-        got = xor_shuffle(jnp.stack(exchange_planes([picked[k] for k in range(E)])), plane)
-        full = got.swapaxes(0, 1).reshape(SLOTS, width)
+        (full,) = run(
+            "join",
+            join_body,
+            [shape((SLOTS, width), BF16)],
+            [at, *exchange_planes([picked[k] for k in range(E)])],
+        )
         full = jnp.stack(gather_subs(full))
-        return gather_narrow(full).reshape(-1, width)
+        two = jnp.stack([full, by_narrow(full, 2)])
+        one = by_narrow(two, 1)
+        return jnp.stack([two[0], one[0], two[1], one[1]]).reshape(-1, width)
 
     grad_rows = dispatch(turned_grad)
     weight_in = expert_in[0]
@@ -364,21 +595,27 @@
         got = by_narrow(jnp.stack([low[1], low[3]]), 1)
         two = jnp.stack([shaped[0], shaped[2]]) + got.astype(F32)
         one = two[0] + by_narrow(two[1].astype(BF16), 2).astype(F32)
-        return reduce_subs([one[j] for j in range(subs)])
-
-    def from_planes(rows, extra=None):
-        pieces = rows.astype(BF16).reshape(SLOTS, E, slice_width).swapaxes(0, 1)
-        pieces = xor_shuffle(pieces, plane)
-        if extra is not None:
-            more = jnp.broadcast_to(extra.astype(BF16)[None], (E,) + extra.shape)
-            pieces = jnp.concatenate([pieces, more], axis=-1)
-        return jnp.stack(exchange_planes([pieces[k] for k in range(E)]))
+        parts, bit = [one[j] for j in range(subs)], subs // 2
+        while bit > 1:
+            parts = [parts[j] + by_sub(parts[j + bit].astype(BF16), bit).astype(F32) for j in range(bit)]
+            bit //= 2
+        return parts[0], by_sub(parts[1].astype(BF16), 1)
+
+    def from_planes(own, got, extra):
+        pieces = run(
+            "split",
+            split_body(extra),
+            [shape((SLOTS, slice_width + extra), BF16)] * E,
+            [at, own, got],
+            [pltpu.VMEM(own.shape, BF16)],
+        )
+        return jnp.stack(exchange_planes(pieces))
 
     returned = give_back(jnp.concatenate([drows, row_stats], axis=1))
-    returned = from_planes(returned[:, :width], returned[:, width:])
+    returned = from_planes(*returned, row_stats.shape[1])
     combined = jnp.einsum("kst,ksd->ktd", select, returned, preferred_element_type=F32)
-    per_expert = xor_shuffle(combined[:, :, slice_width : slice_width + 2], plane)
-    dprob_two = keep_two * jnp.sum(hot_two * per_expert[:, :, 0].T[None], axis=-1)
+    per_expert = combined[:, :, slice_width : slice_width + 2]
+    dprob_two = keep_two * jnp.sum(hot_two_k * per_expert[:, None, :, 0], axis=0)
     inner_two = jnp.sum(per_expert[:, :, 1], axis=0)
     dnormed_two = jnp.sum(combined[:, :, :slice_width], axis=0)
 
@@ -403,66 +640,55 @@
         axis=0,
     )
 
-    wide_grad = widen(dhidden.astype(BF16)).reshape(subs, E * TOK, shard_rows)
-    dcontext_raw = scatter_planes(choose(project(wide_grad, out_parts)))
-    output_grad = reduce_subs(
-        [jnp.stack([dot(wide_grad[j], mixed[e], ((0,), (0,))) for e in range(E)]) for j in range(subs)]
-    )
-    dcontext = (dcontext_raw * gate_one[:, :, None]).astype(BF16)
-    dcontext_rows = dcontext.reshape(TOPK * TOK, head_count, HS)
-    dweights = jnp.einsum("rhc,jhc->hrj", dcontext_rows, value_rows, preferred_element_type=F32)
-    dscores = (probs * (dweights - jnp.sum(probs * dweights, axis=-1, keepdims=True))).astype(BF16)
-    dquery = (
-        jnp.einsum("hrj,jhc->rhc", dscores, key_rows, preferred_element_type=F32) * score_scale
-    ).reshape(TOPK, TOK, local_width)
-    dkeys = (
-        jnp.einsum("hrj,rhc->jhc", dscores, query_rows, preferred_element_type=F32) * score_scale
-    ).reshape(TOK, local_width)
-    dvalues = jnp.einsum(
-        "hrj,rhc->jhc", probs_low, dcontext_rows, preferred_element_type=F32
-    ).reshape(TOK, local_width)
-    dkey_val = jnp.stack([dkeys, dvalues])
-    home_sums = jnp.concatenate(
-        [
-            jnp.sum(context.astype(F32) * dcontext_raw, axis=-1),
-            (
-                jnp.sum(dquery * query.astype(F32), axis=(0, 2))
-                + jnp.sum(dkey_val * key_val.astype(F32), axis=(0, 2))
-            )[None],
-        ],
-        axis=0,
-    )
+    wide_grad, *dcontext_blocks = run(
+        "dcontext",
+        routed_body(subs, False),
+        [shape((rows_all, slice_width), BF16), kept_own] + [sent] * (E - 1),
+        [at, *gather_narrow(dhidden.astype(BF16)), hot_cols, *out_parts],
+        routed_scratch,
+    )
+    dcontext_blocks = exchange_planes(dcontext_blocks)
+
+    def weight_grad(name, rows, other):
+        count, half = other.shape[0], subs // 2
+        parts = run(
+            name,
+            weight_grad_body,
+            [shape((count, shard_rows, local_width), F32 if j < half else BF16) for j in range(subs)],
+            [at, rows, other],
+            [pltpu.VMEM((slice_width, local_width), F32)],
+        )
+        return finish_subs(parts[:half], parts[half:])
+
+    output_grad = weight_grad("output_grad", wide_grad, mixed)
+    dquery_low, dkv_low, home_sums = run(
+        "attention_back",
+        attention_back_body,
+        [sent, sent, shape((8, TOK), F32)],
+        [at, *dcontext_blocks, token_cols, low, probs, context],
+    )
+    (dmixed,) = run(
+        "spread",
+        spread_body,
+        [shape((E, rows_all, local_width), BF16)],
+        [at, *gather_planes(dquery_low), hot_cols],
+    )
+    query_grad = weight_grad("query_grad", gained, dmixed)
     home_sums = sum_narrow(home_sums)
     dprob_one = keep_one * home_sums[:2]
     dlogit_one = gate_back(prob_one, dprob_one, hot_one)
     inner_one = home_sums[2] + jnp.sum(dlogit_one * logits_one, axis=-1)
     dlogit_scaled = dlogit_one * scale_one[:, None]
 
-    dkv_low = (dkey_val * scale_one[None, :, None]).astype(BF16)
-    dkv_all = jnp.stack(gather_planes(dkv_low), axis=1).reshape(2, E * TOK, local_width)
-    dlogit_low = dlogit_scaled.T.astype(BF16)
-    dlogit_rest = (dlogit_scaled.T - dlogit_low.astype(F32)).astype(BF16)
-    dlogit_rows = jnp.concatenate([dlogit_low.reshape(1, -1), dlogit_rest.reshape(1, -1)], axis=0)
-    dquery_low = (dquery * scale_one[None, :, None]).astype(BF16).reshape(TOPK * TOK, local_width)
-    dquery_sent = jnp.concatenate([dquery_low, jnp.pad(dlogit_rows, ((0, 14), (0, 0)))], axis=0)
-    dquery_all = jnp.stack(gather_planes(dquery_sent))
-    dlogit_all = jnp.sum(dquery_all[:, TOPK * TOK : TOPK * TOK + 2].astype(F32), axis=1)
-    dlogit_all = dlogit_all.reshape(E, E, TOK).swapaxes(1, 2).reshape(E * TOK, E)
-    dquery_all = dquery_all[:, : TOPK * TOK].reshape(E, TOPK, TOK, local_width)
-    dmixed = spread(dquery_all)
-
-    kv_grad = reduce_subs(
-        [jnp.stack([dot(gained[j], dkv_all[a], ((0,), (0,))) for a in range(2)]) for j in range(subs)]
-    )
-    query_grad = reduce_subs(
-        [jnp.stack([dot(gained[j], dmixed[e], ((0,), (0,))) for e in range(E)]) for j in range(subs)]
-    )
-    dnormed_one = to_turned(
-        [
-            back([dkv_all[0], dkv_all[1]], kv_parts[j]) + back(dmixed, query_parts[j])
-            for j in range(subs)
-        ]
-    )
+    dkv_all, *dnormed_one = run(
+        "input",
+        input_body(subs),
+        [shape((2, rows_all, local_width), BF16)] + folded,
+        [at, *gather_planes(dkv_low), dmixed, *kv_parts, *query_parts],
+        [pltpu.VMEM((2 + E, slice_width, local_width), BF16)],
+    )
+    kv_grad = weight_grad("key_value_grad", gained, dkv_all)
+    dnormed_one = reduce_narrow(*dnormed_one)
     turned_out = dhidden + dnormed_one * gain_one_plane
     home_out = swap(turned_out.astype(BF16)).astype(F32)
     stream_grad = (
@@ -472,11 +698,9 @@
     )
 
     gain_term = jnp.sum(dnormed_one * turned_stream.astype(F32), axis=0)
-    small = jnp.concatenate([mlp_terms, gain_term[None]], axis=0)
-    small = sum_narrow(small)
-    gained_plane = xor_shuffle(gained, sub).transpose(1, 0, 2).reshape(E * TOK, slice_width)
-    router_term = dot(dlogit_all, gained_plane.astype(F32), ((0,), (0,)), PRECISE)
-    small = sum_subs(jnp.concatenate([small, router_term], axis=0))
+    router_term = swap(dot(dlogit_scaled, gained_home, ((0,), (0,)), PRECISE))
+    small = jnp.concatenate([mlp_terms, gain_term[None], router_term], axis=0)
+    small = sum_subs(sum_narrow(small))
     mine = lax.dynamic_slice_in_dim(small, sub * shard_rows, shard_rows, 1)
     router_one_grad = mine[6:10]
     gain_one_grad = mine[5] + jnp.sum(
@@ -484,7 +708,7 @@
     ) / attn_gain.astype(F32)
 
     expert_out = dot(activation, weight_down, ((1,), (0,))) * row_gate
-    mixture = from_planes(give_back(expert_out))
+    mixture = from_planes(*give_back(expert_out), 0)
     mixture = jnp.einsum("kst,ksd->td", select, mixture, preferred_element_type=F32)
     layer_out = swap((hidden + mixture).astype(BF16)).astype(F32)
     gated_act = (activation.astype(F32) * row_gate).astype(BF16)

time: 570 us -> 539 us (0.946)
  the two profiles are of different devices: /device:TPU:0 before, /device:TPU:2 now
where the time goes in v2:
time: 539 us; the launch traced here: 530 us
  waiting for transfers between devices  181 us (34%)
  starting transfers between devices  138 us (26%)
  Pallas kernels  65.8 us (12%)
  other arithmetic  56.3 us (10%)
  local copies, waits for them, and re-layouts  43.3 us (8%)
  matrix products  42.9 us (8%)
    ppermute x35, waiting for transfers between devices, by_plane(): lax.ppermute(values, 'wide', [(i, i ^ k * subs) for i in range(wide_count)])  89 us
    ppermute x35, starting transfers between devices, by_plane(): lax.ppermute(values, 'wide', [(i, i ^ k * subs) for i in range(wide_count)])  72.7 us
    pallas_call x15, Pallas kernels, run(): pl.pallas_call(body, out_shape=tuple(outs), in_specs=[pl.BlockSpec(memory...  65.8 us
    ppermute x24, waiting for transfers between devices, by_narrow(): lax.ppermute(values, 'narrow', [(i, i ^ k) for i in range(narrow_count)])  46.5 us
    ppermute x12, waiting for transfers between devices, by_sub(): return lax.ppermute(values, 'wide', [(i, i ^ k) for i in range(wide_count)])  45.3 us
    ppermute x5, starting transfers between devices, swap(): return lax.ppermute(values, ('wide', 'narrow'), pairs)  35.2 us
    dot_general x10, matrix products, dot(): lax.dot_general(left, right, ((contract[0], contract[1]), ((), ())), prec...  18.2 us
    ppermute x24, starting transfers between devices, by_narrow(): lax.ppermute(values, 'narrow', [(i, i ^ k) for i in range(narrow_count)])  17.6 us
  transfers between devices with their start and end apart: 76, of which 30 were waited for; matrix products, arithmetic and copies ran while one was open for 21% of the time, Pallas kernels for 10%

profile of v2, /device:TPU:2, one launch (start us, length us, event | category | flops | bytes accessed | tf_op | source)
XLA Modules:
  0.0 529.5 jit_solution(16553278422307640446)
XLA Ops:
  94.3 8.0 %collective-permute-done.7.refs_1_ = bf16[2,128,512]{2,1,0:T(8,128)(2,1)S(1)} collective-permute-done((bf16[2,128,512]{2,1,0:T(8,128)(2,1)}, bf16[2,128,512]{2,1,0:T(8,128)(2,1)S(1)}, u32[]{:S(2)}, u32[]{:S(2)}) %collective-permute-start.7) | collective-permute-done | bytes 262176 | tf_op jit(solution)/shard_map/ppermute | solution.py:320
  105.4 18.4 %collective-permute-start.37 = (bf16[128,512]{1,0:T(8,128)(2,1)}, bf16[128,512]{1,0:T(8,128)(2,1)S(1)}, u32[]{:S(2)}, u32[]{:S(2)}) collective-permute-start(bf16[128,512]{1,0:T(8,128)(2,1)} %param.15), channel_id=1, source_target_pairs={{0,0},{1,8},{2,16},{3,24},{4,4},{5,12},{6,20},{7,28},{8,1},{9,9},{... | collective-permute-start | bytes 393224 | tf_op jit(solution)/shard_map/ppermute | solution.py:334
  124.9 5.3 attention.1
  130.2 7.9 %collective-permute-start.18 = (bf16[2,128,512]{2,1,0:T(8,128)(2,1)}, bf16[2,128,512]{2,1,0:T(8,128)(2,1)S(1)}, u32[]{:S(2)}, u32[]{:S(2)}) collective-permute-start(bf16[2,128,512]{2,1,0:T(8,128)(2,1)} %get-tuple-element.63.refs_0_), channel_id=1, source_target_pairs={{0,8},{4,12},{8,0},{12,4},{16,24},{20,28},{24,16},{28,20},{1,9},{5... | collective-permute-start | bytes 786440 | tf_op jit(solution)/shard_map/ppermute | solution.py:320
  152.1 11.2 %collective-permute-done.19.refs_2_ = bf16[2,128,512]{2,1,0:T(8,128)(2,1)} collective-permute-done((bf16[2,128,512]{2,1,0:T(8,128)(2,1)}, bf16[2,128,512]{2,1,0:T(8,128)(2,1)}, u32[]{:S(2)}, u32[]{:S(2)}) %collective-permute-start.19) | collective-permute-done | bytes 262176 | tf_op jit(solution)/shard_map/ppermute | solution.py:320
  185.6 6.1 %collective-permute-start.24 = (bf16[80,512]{1,0:T(8,128)(2,1)S(1)}, bf16[80,512]{1,0:T(8,128)(2,1)S(1)}, u32[]{:S(2)}, u32[]{:S(2)}) collective-permute-start(bf16[80,512]{1,0:T(8,128)(2,1)S(1)} %get-tuple-element.144), channel_id=1, source_target_pairs={{0,8},{4,12},{8,0},{12,4},{16,24},{20,28},{24,16},{28,20},{1,9},{5... | collective-permute-start | bytes 245768 | tf_op jit(solution)/shard_map/ppermute | solution.py:320
  204.3 6.6 %collective-permute-start.39 = (f32[5,128]{1,0:T(8,128)S(1)}, f32[5,128]{1,0:T(8,128)S(1)}, u32[]{:S(2)}, u32[]{:S(2)}) collective-permute-start(f32[5,128]{1,0:T(8,128)S(1)} %fusion.129), channel_id=1, source_target_pairs={{0,16},{4,20},{8,24},{12,28},{16,0},{20,4},{24,8},{28,12},{1,17},{... | collective-permute-start | bytes 7688 | tf_op jit(solution)/shard_map/ppermute | solution.py:320
  214.7 15.0 %collective-permute-done.28 = bf16[2,80,2048]{2,1,0:T(8,128)(2,1)S(1)} collective-permute-done((bf16[2,80,2048]{2,1,0:T(8,128)(2,1)S(1)}, bf16[2,80,2048]{2,1,0:T(8,128)(2,1)S(1)}, u32[]{:S(2)}, u32[]{:S(2)}) %collective-permute-start.28) | collective-permute-done | bytes 655392 | tf_op jit(solution)/shard_map/ppermute | solution.py:326
  241.0 6.7 %fusion.11 = f32[2,640,704]{1,2,0:T(8,128)S(1)} fusion(bf16[640,2048,1]{1,0,2:T(8,128)(2,1)S(1)} %bitcast.393, bf16[1,2048,2,704]{1,3,2,0:T(8,128)(2,1)} %param.23), kind=kOutput, calls=%fused_computation.28 | convolution fusion | flops 3690987520 | bytes 11993088 | tf_op jit(solution)/shard_map/rd,dkf->krf/dot_general | solution.py:573
  265.8 13.8 %collective-permute-done.47 = bf16[2,80,2176]{2,1,0:T(8,128)(2,1)S(1)} collective-permute-done((bf16[2,80,2176]{2,1,0:T(8,128)(2,1)S(1)}, bf16[2,80,2176]{2,1,0:T(8,128)(2,1)S(1)}, u32[]{:S(2)}, u32[]{:S(2)}) %collective-permute-start.47) | collective-permute-done | bytes 696352 | tf_op jit(solution)/shard_map/ppermute | solution.py:326
  281.8 7.8 %collective-permute-done.48.got = bf16[80,2176]{1,0:T(8,128)(2,1)} collective-permute-done((bf16[80,2176]{1,0:T(8,128)(2,1)S(1)}, bf16[80,2176]{1,0:T(8,128)(2,1)}, u32[]{:S(2)}, u32[]{:S(2)}) %collective-permute-start.48) | collective-permute-done | bytes 348192 | tf_op jit(solution)/shard_map/ppermute | solution.py:323
  289.6 10.5 %split.3 = (bf16[80,640]{1,0:T(8,128)(2,1)}, bf16[80,640]{1,0:T(8,128)(2,1)}, bf16[80,640]{1,0:T(8,128)(2,1)}, bf16[80,640]{1,0:T(8,128)(2,1)}) custom-call(s32[4]{0:T(128)} %pad_add_fusion.at, f32[80,2176]{1,0:T(8,128)} %slice_bitcast_fusion.2.own, bf16[80,2176]{1,0:T(8,128)(2,1)} %collective-permute-done.48.got), custom_call_target="tpu_custom_call" | custom-call | tf_op jit(solution)/shard_map/split/pallas_call | solution.py:52
  301.7 7.0 %collective-permute-start.50 = (bf16[80,640]{1,0:T(8,128)(2,1)}, bf16[80,640]{1,0:T(8,128)(2,1)S(1)}, u32[]{:S(2)}, u32[]{:S(2)}) collective-permute-start(bf16[80,640]{1,0:T(8,128)(2,1)} %get-tuple-element.73), channel_id=1, source_target_pairs={{0,16},{4,20},{8,24},{12,28},{16,0},{20,4},{24,8},{28,12},{1,17},{... | collective-permute-start | bytes 307208 | tf_op jit(solution)/shard_map/ppermute | solution.py:320
  319.6 5.3 %collective-permute-done.31 = bf16[2,80,2048]{2,1,0:T(8,128)(2,1)S(1)} collective-permute-done((bf16[2,80,2048]{2,1,0:T(8,128)(2,1)S(1)}, bf16[2,80,2048]{2,1,0:T(8,128)(2,1)S(1)}, u32[]{:S(2)}, u32[]{:S(2)}) %collective-permute-start.31) | collective-permute-done | bytes 655392 | tf_op jit(solution)/shard_map/ppermute | solution.py:326
  347.9 12.8 %collective-permute-done.56.refs_1_ = bf16[2,128,512]{2,1,0:T(8,128)(2,1)} collective-permute-done((bf16[2,128,512]{2,1,0:T(8,128)(2,1)}, bf16[2,128,512]{2,1,0:T(8,128)(2,1)}, u32[]{:S(2)}, u32[]{:S(2)}) %collective-permute-start.56) | collective-permute-done | bytes 262176 | tf_op jit(solution)/shard_map/ppermute | solution.py:320
  365.6 6.2 %collective-permute-start.61 = (bf16[2,128,512]{2,1,0:T(8,128)(2,1)}, bf16[2,128,512]{2,1,0:T(8,128)(2,1)S(1)}, u32[]{:S(2)}, u32[]{:S(2)}) collective-permute-start(bf16[2,128,512]{2,1,0:T(8,128)(2,1)} %get-tuple-element.83.refs_0_), channel_id=1, source_target_pairs={{0,8},{4,12},{8,0},{12,4},{16,24},{20,28},{24,16},{28,20},{1,9},{5... | collective-permute-start | bytes 786440 | tf_op jit(solution)/shard_map/ppermute | solution.py:320
  373.6 8.9 %convolution_bitcast_fusion = f32[1,2048,2,704]{1,3,2,0:T(8,128)} fusion(bf16[640,2048,1]{1,0,2:T(8,128)(2,1)S(1)} %bitcast.394, bf16[640,1,704]{0,2,1:T(8,128)(2,1)} %get-tuple-element.119, bf16[640,1,704]{0,2,1:T(8,128)(2,1)} %get-tuple-element.107), kind=kOutput, calls=%fused_computation.11 | convolution fusion | flops 3694592000 | bytes 15958016 | tf_op jit(solution)/shard_map/rd,rkf->dkf/dot_general | solution.py:723
  390.8 37.8 %collective-permute-done.62.refs_2_ = bf16[2,128,512]{2,1,0:T(8,128)(2,1)S(1)} collective-permute-done((bf16[2,128,512]{2,1,0:T(8,128)(2,1)S(1)}, bf16[2,128,512]{2,1,0:T(8,128)(2,1)S(1)}, u32[]{:S(2)}, u32[]{:S(2)}) %collective-permute-start.62) | collective-permute-done | bytes 262176 | tf_op jit(solution)/shard_map/ppermute | solution.py:320
  435.8 5.8 %input.1 = (bf16[2,512,512]{2,1,0:T(8,128)(2,1)}, f32[128,512]{1,0:T(8,128)}, f32[128,512]{1,0:T(8,128)}, bf16[2,128,512]{2,1,0:T(8,128)(2,1)}) custom-call(s32[4]{0:T(128)} %pad_add_fusion.at, bf16[2,128,512]{2,1,0:T(8,128)(2,1)} %get-tuple-element.82.refs_0_, bf16[2,128,512]{2,1,0:T(8,128)(2,1)} %copy-done.27, bf16[2,128,512]{2,1,0:T(8,128)(2,1)} %copy-done.28, ...), custom_call_target="tpu_custom_call" | custom-call | tf_op jit(solution)/shard_map/input/pallas_call | solution.py:52
  446.9 5.2 collective-permute-start.69
  455.0 4.9 convolution_bitcast_fusion.1
  470.5 5.0 query_grad.1
  485.8 7.5 %collective-permute-done.72 = f32[10,512]{1,0:T(8,128)S(1)} collective-permute-done((f32[10,512]{1,0:T(8,128)S(1)}, f32[10,512]{1,0:T(8,128)S(1)}, u32[]{:S(2)}, u32[]{:S(2)}) %collective-permute-start.72) | collective-permute-done | bytes 20512 | tf_op jit(solution)/shard_map/ppermute | solution.py:323
  505.7 21.1 %collective-permute-done.74 = bf16[4,256,512]{2,1,0:T(8,128)(2,1)S(1)} collective-permute-done((bf16[4,256,512]{2,1,0:T(8,128)(2,1)}, bf16[4,256,512]{2,1,0:T(8,128)(2,1)S(1)}, u32[]{:S(2)}, u32[]{:S(2)}) %collective-permute-start.74) | collective-permute-done | bytes 1048608 | tf_op jit(solution)/shard_map/ppermute | solution.py:323
  (527 shorter events, 282.3 us)
Async XLA Ops:
  0.7 67.3 %collective-permute-start = (bf16[128,512]{1,0:T(8,128)(2,1)}, bf16[128,512]{1,0:T(8,128)(2,1)}, u32[]{:S(2)}, u32[]{:S(2)}) collective-permute-start(bf16[128,512]{1,0:T(8,128)(2,1)} %param.14), channel_id=1, source_target_pairs={{0,0},{1,8},{2,16},{3,24},{4,4},{5,12},{6,20},{7,28},{8,1},{9,9},{... | collective-permute-start | bytes 393224 | tf_op jit(solution)/shard_map/ppermute | solution.py:334
  10.6 64.9 %collective-permute-start.5 = (bf16[2,256,512]{2,1,0:T(8,128)(2,1)}, bf16[2,256,512]{2,1,0:T(8,128)(2,1)S(1)}, u32[]{:S(2)}, u32[]{:S(2)}) collective-permute-start(bf16[2,256,512]{2,1,0:T(8,128)(2,1)} %refs_5_.7), channel_id=1, source_target_pairs={{0,4},{4,0},{8,12},{12,8},{16,20},{20,16},{24,28},{28,24},{1,5},{5... | collective-permute-start | bytes 1572872 | tf_op jit(solution)/shard_map/ppermute | solution.py:323
  21.8 64.2 %collective-permute-start.12 = (bf16[4,256,512]{2,1,0:T(8,128)(2,1)}, bf16[4,256,512]{2,1,0:T(8,128)(2,1)}, u32[]{:S(2)}, u32[]{:S(2)}) collective-permute-start(bf16[4,256,512]{2,1,0:T(8,128)(2,1)} %refs_7_.1), channel_id=1, source_target_pairs={{0,4},{4,0},{8,12},{12,8},{16,20},{20,16},{24,28},{28,24},{1,5},{5... | collective-permute-start | bytes 3145736 | tf_op jit(solution)/shard_map/ppermute | solution.py:323
  23.3 119.8 %collective-permute-start.21 = (bf16[4,256,512]{2,1,0:T(8,128)(2,1)}, bf16[4,256,512]{2,1,0:T(8,128)(2,1)}, u32[]{:S(2)}, u32[]{:S(2)}) collective-permute-start(bf16[4,256,512]{2,1,0:T(8,128)(2,1)} %refs_5_.6), channel_id=1, source_target_pairs={{0,4},{4,0},{8,12},{12,8},{16,20},{20,16},{24,28},{28,24},{1,5},{5... | collective-permute-start | bytes 3145736 | tf_op jit(solution)/shard_map/ppermute | solution.py:323
  90.4 34.2 %collective-permute-start.13 = (bf16[2,128,512]{2,1,0:T(8,128)(2,1)}, bf16[2,128,512]{2,1,0:T(8,128)(2,1)}, u32[]{:S(2)}, u32[]{:S(2)}) collective-permute-start(bf16[2,128,512]{2,1,0:T(8,128)(2,1)} %get-tuple-element.60), channel_id=1, source_target_pairs={{0,8},{4,12},{8,0},{12,4},{16,24},{20,28},{24,16},{28,20},{1,9},{5... | collective-permute-start | bytes 786440 | tf_op jit(solution)/shard_map/ppermute | solution.py:320
  94.1 30.8 %collective-permute-start.14 = (bf16[2,128,512]{2,1,0:T(8,128)(2,1)}, bf16[2,128,512]{2,1,0:T(8,128)(2,1)}, u32[]{:S(2)}, u32[]{:S(2)}) collective-permute-start(bf16[2,128,512]{2,1,0:T(8,128)(2,1)} %get-tuple-element.61), channel_id=1, source_target_pairs={{0,16},{4,20},{8,24},{12,28},{16,0},{20,4},{24,8},{28,12},{1,17},{... | collective-permute-start | bytes 786440 | tf_op jit(solution)/shard_map/ppermute | solution.py:320
  105.4 36.2 %collective-permute-start.37 = (bf16[128,512]{1,0:T(8,128)(2,1)}, bf16[128,512]{1,0:T(8,128)(2,1)S(1)}, u32[]{:S(2)}, u32[]{:S(2)}) collective-permute-start(bf16[128,512]{1,0:T(8,128)(2,1)} %param.15), channel_id=1, source_target_pairs={{0,0},{1,8},{2,16},{3,24},{4,4},{5,12},{6,20},{7,28},{8,1},{9,9},{... | collective-permute-start | bytes 393224 | tf_op jit(solution)/shard_map/ppermute | solution.py:334
  138.2 25.1 %collective-permute-start.19 = (bf16[2,128,512]{2,1,0:T(8,128)(2,1)}, bf16[2,128,512]{2,1,0:T(8,128)(2,1)}, u32[]{:S(2)}, u32[]{:S(2)}) collective-permute-start(bf16[2,128,512]{2,1,0:T(8,128)(2,1)} %get-tuple-element.63.refs_0_), channel_id=1, source_target_pairs={{0,16},{4,20},{8,24},{12,28},{16,0},{20,4},{24,8},{28,12},{1,17},{... | collective-permute-start | bytes 786440 | tf_op jit(solution)/shard_map/ppermute | solution.py:320
  142.5 25.7 %collective-permute-start.40 = (bf16[80,512]{1,0:T(8,128)(2,1)}, bf16[80,512]{1,0:T(8,128)(2,1)}, u32[]{:S(2)}, u32[]{:S(2)}) collective-permute-start(bf16[80,512]{1,0:T(8,128)(2,1)} %get-tuple-element.140), channel_id=1, source_target_pairs={{0,8},{4,12},{8,0},{12,4},{16,24},{20,28},{24,16},{28,20},{1,9},{5... | collective-permute-start | bytes 245768 | tf_op jit(solution)/shard_map/ppermute | solution.py:320
  143.1 25.7 %collective-permute-start.41 = (bf16[80,512]{1,0:T(8,128)(2,1)}, bf16[80,512]{1,0:T(8,128)(2,1)}, u32[]{:S(2)}, u32[]{:S(2)}) collective-permute-start(bf16[80,512]{1,0:T(8,128)(2,1)} %get-tuple-element.139), channel_id=1, source_target_pairs={{0,16},{4,20},{8,24},{12,28},{16,0},{20,4},{24,8},{28,12},{1,17},{... | collective-permute-start | bytes 245768 | tf_op jit(solution)/shard_map/ppermute | solution.py:320
  198.7 31.3 %collective-permute-start.45 = (bf16[2,2,80,2048]{3,2,1,0:T(8,128)(2,1)}, bf16[2,2,80,2048]{3,2,1,0:T(8,128)(2,1)}, u32[]{:S(2)}, u32[]{:S(2)}) collective-permute-start(bf16[2,2,80,2048]{3,2,1,0:T(8,128)(2,1)} %pad_maximum_fusion.6), channel_id=1, source_target_pairs={{0,1},{1,0},{2,3},{3,2},{4,5},{5,4},{6,7},{7,6},{8,9},{9,8},{10,11... | collective-permute-start | bytes 3932168 | tf_op jit(solution)/shard_map/ppermute | solution.py:326
  335.5 25.2 %collective-permute-start.56 = (bf16[2,128,512]{2,1,0:T(8,128)(2,1)}, bf16[2,128,512]{2,1,0:T(8,128)(2,1)}, u32[]{:S(2)}, u32[]{:S(2)}) collective-permute-start(bf16[2,128,512]{2,1,0:T(8,128)(2,1)} %get-tuple-element.77), channel_id=1, source_target_pairs={{0,16},{4,20},{8,24},{12,28},{16,0},{20,4},{24,8},{28,12},{1,17},{... | collective-permute-start | bytes 786440 | tf_op jit(solution)/shard_map/ppermute | solution.py:320
  341.5 41.0 %collective-permute-start.35 = (bf16[80,512]{1,0:T(8,128)(2,1)}, bf16[80,512]{1,0:T(8,128)(2,1)}, u32[]{:S(2)}, u32[]{:S(2)}) collective-permute-start(bf16[80,512]{1,0:T(8,128)(2,1)} %get-tuple-element.70), channel_id=1, source_target_pairs={{0,24},{4,28},{8,16},{12,20},{16,8},{20,12},{24,0},{28,4},{1,25},{... | collective-permute-start | bytes 245768 | tf_op jit(solution)/shard_map/ppermute | solution.py:320
  343.9 38.7 %collective-permute-start.34 = (bf16[80,512]{1,0:T(8,128)(2,1)}, bf16[80,512]{1,0:T(8,128)(2,1)}, u32[]{:S(2)}, u32[]{:S(2)}) collective-permute-start(bf16[80,512]{1,0:T(8,128)(2,1)} %get-tuple-element.69), channel_id=1, source_target_pairs={{0,16},{4,20},{8,24},{12,28},{16,0},{20,4},{24,8},{28,12},{1,17},{... | collective-permute-start | bytes 245768 | tf_op jit(solution)/shard_map/ppermute | solution.py:320
  347.9 34.7 %collective-permute-start.33 = (bf16[80,512]{1,0:T(8,128)(2,1)}, bf16[80,512]{1,0:T(8,128)(2,1)}, u32[]{:S(2)}, u32[]{:S(2)}) collective-permute-start(bf16[80,512]{1,0:T(8,128)(2,1)} %get-tuple-element.68), channel_id=1, source_target_pairs={{0,8},{4,12},{8,0},{12,4},{16,24},{20,28},{24,16},{28,20},{1,9},{5... | collective-permute-start | bytes 245768 | tf_op jit(solution)/shard_map/ppermute | solution.py:320
  384.5 49.9 %collective-permute-start.58 = (bf16[2,128,512]{2,1,0:T(8,128)(2,1)}, bf16[2,128,512]{2,1,0:T(8,128)(2,1)S(1)}, u32[]{:S(2)}, u32[]{:S(2)}) collective-permute-start(bf16[2,128,512]{2,1,0:T(8,128)(2,1)} %get-tuple-element.82.refs_0_), channel_id=1, source_target_pairs={{0,8},{4,12},{8,0},{12,4},{16,24},{20,28},{24,16},{28,20},{1,9},{5... | collective-permute-start | bytes 786440 | tf_op jit(solution)/shard_map/ppermute | solution.py:320
  384.5 49.9 %collective-permute-start.59 = (bf16[2,128,512]{2,1,0:T(8,128)(2,1)}, bf16[2,128,512]{2,1,0:T(8,128)(2,1)S(1)}, u32[]{:S(2)}, u32[]{:S(2)}) collective-permute-start(bf16[2,128,512]{2,1,0:T(8,128)(2,1)} %get-tuple-element.82.refs_0_), channel_id=1, source_target_pairs={{0,16},{4,20},{8,24},{12,28},{16,0},{20,4},{24,8},{28,12},{1,17},{... | collective-permute-start | bytes 786440 | tf_op jit(solution)/shard_map/ppermute | solution.py:320
  386.3 49.5 %collective-permute-start.60 = (bf16[2,128,512]{2,1,0:T(8,128)(2,1)}, bf16[2,128,512]{2,1,0:T(8,128)(2,1)}, u32[]{:S(2)}, u32[]{:S(2)}) collective-permute-start(bf16[2,128,512]{2,1,0:T(8,128)(2,1)} %get-tuple-element.82.refs_0_), channel_id=1, source_target_pairs={{0,24},{4,28},{8,16},{12,20},{16,8},{20,12},{24,0},{28,4},{1,25},{... | collective-permute-start | bytes 786440 | tf_op jit(solution)/shard_map/ppermute | solution.py:320
  388.9 39.6 %collective-permute-start.62 = (bf16[2,128,512]{2,1,0:T(8,128)(2,1)S(1)}, bf16[2,128,512]{2,1,0:T(8,128)(2,1)S(1)}, u32[]{:S(2)}, u32[]{:S(2)}) collective-permute-start(bf16[2,128,512]{2,1,0:T(8,128)(2,1)S(1)} %copy-done.22), channel_id=1, source_target_pairs={{0,16},{4,20},{8,24},{12,28},{16,0},{20,4},{24,8},{28,12},{1,17},{... | collective-permute-start | bytes 786440 | tf_op jit(solution)/shard_map/ppermute | solution.py:320
  388.9 41.5 %collective-permute-start.63 = (bf16[2,128,512]{2,1,0:T(8,128)(2,1)S(1)}, bf16[2,128,512]{2,1,0:T(8,128)(2,1)S(1)}, u32[]{:S(2)}, u32[]{:S(2)}) collective-permute-start(bf16[2,128,512]{2,1,0:T(8,128)(2,1)S(1)} %copy-done.22), channel_id=1, source_target_pairs={{0,24},{4,28},{8,16},{12,20},{16,8},{20,12},{24,0},{28,4},{1,25},{... | collective-permute-start | bytes 786440 | tf_op jit(solution)/shard_map/ppermute | solution.py:320
  428.6 31.4 %collective-permute-start.36 = (bf16[128,512]{1,0:T(8,128)(2,1)}, bf16[128,512]{1,0:T(8,128)(2,1)}, u32[]{:S(2)}, u32[]{:S(2)}) collective-permute-start(bf16[128,512]{1,0:T(8,128)(2,1)} %fusion.30), channel_id=1, source_target_pairs={{0,0},{1,8},{2,16},{3,24},{4,4},{5,12},{6,20},{7,28},{8,1},{9,9},{... | collective-permute-start | bytes 393224 | tf_op jit(solution)/shard_map/ppermute | solution.py:334
  466.4 28.7 %collective-permute-start.75 = (bf16[4,256,512]{2,1,0:T(8,128)(2,1)}, bf16[4,256,512]{2,1,0:T(8,128)(2,1)}, u32[]{:S(2)}, u32[]{:S(2)}) collective-permute-start(bf16[4,256,512]{2,1,0:T(8,128)(2,1)} %get-tuple-element.96), channel_id=1, source_target_pairs={{0,4},{4,0},{8,12},{12,8},{16,20},{20,16},{24,28},{28,24},{1,5},{5... | collective-permute-start | bytes 3145736 | tf_op jit(solution)/shard_map/ppermute | solution.py:323
  478.8 25.7 %collective-permute-start.73 = (bf16[2,256,512]{2,1,0:T(8,128)(2,1)}, bf16[2,256,512]{2,1,0:T(8,128)(2,1)S(1)}, u32[]{:S(2)}, u32[]{:S(2)}) collective-permute-start(bf16[2,256,512]{2,1,0:T(8,128)(2,1)} %get-tuple-element.90), channel_id=1, source_target_pairs={{0,4},{4,0},{8,12},{12,8},{16,20},{20,16},{24,28},{28,24},{1,5},{5... | collective-permute-start | bytes 1572872 | tf_op jit(solution)/shard_map/ppermute | solution.py:323
  479.8 47.0 %collective-permute-start.74 = (bf16[4,256,512]{2,1,0:T(8,128)(2,1)}, bf16[4,256,512]{2,1,0:T(8,128)(2,1)S(1)}, u32[]{:S(2)}, u32[]{:S(2)}) collective-permute-start(bf16[4,256,512]{2,1,0:T(8,128)(2,1)} %get-tuple-element.92), channel_id=1, source_target_pairs={{0,4},{4,0},{8,12},{12,8},{16,20},{20,16},{24,28},{28,24},{1,5},{5... | collective-permute-start | bytes 3145736 | tf_op jit(solution)/shard_map/ppermute | solution.py:323
  (152 other events, 1980.1 us)
